TPU v7x, 32 devices: a whole 2x2x4 slice. The times are simulated.
32 devices in a mesh: ctx: 16 (over z, y, x), head: 2 (over core).
Axes of the slice: x: 2, y: 2, z: 4, core: 2. Of those that a mesh axis runs over, the one named last changes fastest.
Arguments:
- queries: bfloat16 [2, 4096, 4096], P(None, 'ctx', 'head'), may hold values from -6 to 6
- keys: bfloat16 [2, 4096, 4096], P(None, 'ctx', 'head'), may hold values from -6 to 6
- values: bfloat16 [2, 4096, 4096], P(None, 'ctx', 'head'), may hold values from -6 to 6
- token_gate: float32 [2, 32, 4096], P(None, 'head', 'ctx'), may hold values from 0.2 to 1
- head_rate: float32 [32], P('head'), may hold values from 5.722046e-07 to 0.001953125
- init_state: float32 [32, 128, 128], P('head'), may hold values from -0.53033006 to 0.53033006
- norm_gain: float32 [4096], P('head'), may hold values from 0.5 to 1.5
- out_proj: bfloat16 [4096, 4096], P('head'), may hold values from -0.09375 to 0.09375
- plan: int32 [2], replicated, may hold values from 0 to 1, each once
Outputs:
- layer_out: bfloat16 [4096, 2, 4096], P(('ctx', 'head'))
Inputs may be any that keep to these rules, and one draw needn't show every extreme that they name: `plan`: each sequence appears exactly once.
All inputs are finite; a program needn't handle non-finite values.
Results may differ from a plain program's by a relative error of at most 0.0049.
Values sent between devices are 32-bit elements; how exact they have to be, the bound alone decides.
No kernel may reach another device: no remote copies, remote signals or barrier semaphores. Data moves between devices by JAX's collectives and lax.ppermute only.
A program may use at most 128 MiB of HBM per device.

v0:
```python
import functools

import jax
import jax.numpy as jnp
from jax import lax
from jax.experimental import pallas as pl
from jax.experimental.pallas import tpu as pltpu
from jax.sharding import PartitionSpec as P


HS = 128
MB = 64
EPS = 1e-06
STEP = 8
WIDE = 512
SMALL = 14
LARGE = 30
UP_PERMUTE = (False, True)
DOWN_PERMUTE = (False, True)
F32 = jnp.float32
BF16 = jnp.bfloat16


def mm(a, b, dims=((1,), (0,))):
    return lax.dot_general(a, b, (dims, ((), ())), preferred_element_type=F32)


ROWS_BY_ROWS = ((1,), (1,))


def iotas(rows, cols):
    return tuple(lax.broadcasted_iota(jnp.int32, (rows, cols), axis) for axis in (0, 1))


def eta_rows(gate_ref, rate_ref, heads_step, sign):
    first = pl.program_id(0) * heads_step
    return [gate_ref[0, pl.ds(first + h, 1), :] * (sign * rate_ref[first + h]) for h in range(heads_step)]


def maps_kernel(heads_step, per, plan_ref, rot_ref, k_ref, v_ref, gate_ref, rate_ref, map_ref, t_ref):
    rows = k_ref.shape[1]
    pair = 2 * MB
    each = range(heads_step)
    etas = eta_rows(gate_ref, rate_ref, heads_step, 1.0)
    to, of = iotas(MB, pair)
    left, diag = of < MB, of == to + MB
    eye = jnp.where(jnp.equal(*iotas(pair, pair)), 1.0, 0.0).astype(BF16)
    ks = [k_ref[0, :, h * HS : (h + 1) * HS] for h in each]
    for h in each:
        t_ref[h] = jnp.concatenate([ks[h], -v_ref[0, :, h * HS : (h + 1) * HS]], axis=1)
    for begin in range(0, rows, pair):
        end, late = begin + pair, begin + MB
        if begin:
            reach = [-mm(ks[h][begin:end], ks[h][:begin], ROWS_BY_ROWS) * etas[h][:, :begin] for h in each]
            reach = [jnp.concatenate([r.astype(BF16), eye], axis=1) for r in reach]
            for h in each:
                t_ref[h, begin:end] = mm(reach[h], t_ref[h, :end]).astype(BF16)
        near = [-mm(ks[h][late:end], ks[h][begin:end], ROWS_BY_ROWS) * etas[h][:, begin:end] for h in each]
        near = [jnp.where(left, n, jnp.where(diag, 1.0, 0.0)).astype(BF16) for n in near]
        for h in each:
            t_ref[h, late:end] = mm(near[h], t_ref[h, begin:end]).astype(BF16)
    weighted = [(jnp.transpose(ks[h].astype(F32)) * etas[h]).astype(BF16) for h in each]
    for h in each:
        total = mm(weighted[h], t_ref[h])
        place = lax.rem(rot_ref[0], heads_step // per) ^ (h // per)
        map_ref[place, h % per, 0] = total[:, :HS]
        map_ref[place, h % per, 1] = total[:, HS:]


def reads_kernel(heads_step, plan_ref, q_ref, k_ref, gate_ref, rate_ref, t_ref, less_ref, rest_ref):
    rows = q_ref.shape[1]
    pair = 2 * MB
    each = range(heads_step)
    etas = eta_rows(gate_ref, rate_ref, heads_step, -1.0)
    lower = jnp.greater_equal(*iotas(pair, pair))
    for begin in range(0, rows, pair):
        end = begin + pair
        scores = []
        for h in each:
            cols = slice(h * HS, (h + 1) * HS)
            score = mm(q_ref[0, begin:end, cols], k_ref[0, :end, cols], ROWS_BY_ROWS) * etas[h][:, :end]
            parts = [score[:, :begin]] if begin else []
            parts.append(jnp.where(lower, score[:, begin:], 0.0))
            scores.append(jnp.concatenate(parts, axis=1).astype(BF16))
        for h in each:
            cols = slice(h * HS, (h + 1) * HS)
            taken = mm(scores[h], t_ref[h, :end])
            less_ref[begin:end, cols] = taken[:, :HS].astype(BF16)
            rest_ref[begin:end, cols] = taken[:, HS:]


def advance(state, both):
    return state - mm(both[0].astype(BF16), state.astype(BF16)) - both[1]


def chain_kernel(group, hops, all_out, info_ref, *refs):
    maps, (start_ref, moved_ref), out_ref, held = refs[:group], refs[group:-2], refs[-2], refs[-1]
    rot = info_ref[0]
    for d in range(group):
        held[d ^ rot] = maps[d][0]
    per = held.shape[1]
    states = [start_ref[u] for u in range(per)]
    if hops:
        states = [jnp.where(info_ref[1] == 0, states[u], moved_ref[u]) for u in range(per)]
    for m in range(group):
        for u in range(per):
            if all_out:
                out_ref[m ^ info_ref[3], u] = states[u]
            if not all_out or m < group - 1:
                states[u] = advance(states[u], held[m, u])
    if not all_out:
        for u in range(per):
            out_ref[u] = states[u]


def final_kernel(steps, parts, group, plan_ref, me_ref, rot_ref, q_ref, less_ref, rest_ref, gain_ref, proj_ref, *refs):
    states, outs, (held, normed, proj, sems) = refs[:group], refs[group:-4], refs[-4:]
    piece = normed.shape[1] // parts
    i = pl.program_id(0)
    per = held.shape[1]

    wide = proj.shape[3]

    def chunk(c):
        part = proj_ref.at[:, :, pl.ds(pl.multiple_of(c * wide, wide), wide)]
        return pltpu.make_async_copy(part, proj.at[c], sems.at[c])

    @pl.when(i == 0)
    def _():
        for c in range(proj.shape[0]):
            chunk(c).start()
        for d in range(group):
            held[d ^ rot_ref[0]] = states[d][0]

    @pl.when(i < steps)
    def _():
        heads_step = normed.shape[2] // HS
        zs = []
        for h in range(heads_step):
            cols = slice(h * HS, (h + 1) * HS)
            state = held[i * (heads_step // per) + h // per, h % per]
            main = state.astype(BF16)
            small = (state - main.astype(F32)).astype(BF16)
            q = q_ref[0, :, cols]
            z = mm(jnp.concatenate([q, less_ref[:, cols]], axis=1), jnp.concatenate([main, main], axis=0))
            zs.append(z + mm(q, small) + rest_ref[:, cols])
        for h in range(heads_step):
            cols = slice(h * HS, (h + 1) * HS)
            scale = lax.rsqrt(jnp.mean(zs[h] * zs[h], axis=-1, keepdims=True) + EPS)
            out = (zs[h] * scale * gain_ref[:, cols]).astype(BF16)
            for p in range(parts):
                begin = pl.multiple_of((me_ref[0] ^ p) * piece, piece)
                normed[i, pl.ds(begin, piece), cols] = out[p * piece : (p + 1) * piece]

    @pl.when(i >= steps)
    def _():
        chunk(i - steps).wait()
        product = sum(mm(normed[n], proj[i - steps, n]) for n in range(steps))
        for d in range(parts):
            outs[d][...] = product[d * piece : (d + 1) * piece]


def in_hbm(x):
    return pltpu.with_memory_space_constraint(x, pltpu.HBM)


def in_vmem(x):
    return pltpu.with_memory_space_constraint(x, pltpu.VMEM)


def limit(mib):
    return pltpu.CompilerParams(vmem_limit_bytes=mib * 2**20)


def cost(flops, nbytes):
    return pl.CostEstimate(flops=int(flops), bytes_accessed=int(nbytes), transcendentals=0)


def per_device(queries, keys, values, token_gate, head_rate, init_state, norm_gain, out_proj, plan):
    seqs, rows, width = queries.shape
    heads = init_state.shape[0]
    model = out_proj.shape[1]
    ctx, parts = lax.axis_size("ctx"), lax.axis_size("head")
    plan, head_rate = in_hbm(plan), in_hbm(head_rate)
    group = 1
    while group < 8 and heads % (2 * group) == 0 and ctx % (2 * group) == 0:
        group *= 2
    per = heads // group
    groups = [list(range(g, g + group)) for g in range(0, ctx, group)]
    onward = [(i, i + group) for i in range(ctx - group)]
    position = lax.axis_index("ctx").astype(jnp.int32)
    place, block = lax.rem(position, group), lax.div(position, group)
    rots = {True: place.reshape(1), False: jnp.zeros((1,), jnp.int32)}
    me = lax.axis_index("head").astype(jnp.int32).reshape(1)
    step = STEP if heads % STEP == 0 else heads
    smem = pl.BlockSpec(memory_space=pltpu.SMEM)

    def seq_block(s):
        return pl.BlockSpec((1, rows, step * HS), lambda i, plan_ref: (plan_ref[s], 0, i))

    def gate_block(s):
        return pl.BlockSpec((1, heads, rows), lambda i, plan_ref: (plan_ref[s], 0, 0))

    t_block = pl.BlockSpec((step, rows, 2 * HS), lambda i, plan_ref: (i, 0, 0))
    col_block = pl.BlockSpec((rows, step * HS), lambda i, plan_ref: (0, i))

    def maps_of(s):
        part = step // per
        grid_spec = pltpu.PrefetchScalarGridSpec(
            num_scalar_prefetch=2,
            grid=(heads // step,),
            in_specs=[
                pl.BlockSpec((1, rows, step * HS), lambda i, plan_ref, rot_ref: (plan_ref[s], 0, i)),
                pl.BlockSpec((1, rows, step * HS), lambda i, plan_ref, rot_ref: (plan_ref[s], 0, i)),
                pl.BlockSpec((1, heads, rows), lambda i, plan_ref, rot_ref: (plan_ref[s], 0, 0)),
                smem,
            ],
            out_specs=[
                pl.BlockSpec(
                    (part, per, 2, HS, HS),
                    lambda i, plan_ref, rot_ref: (lax.div(rot_ref[0], part) ^ i, 0, 0, 0, 0),
                ),
                pl.BlockSpec((step, rows, 2 * HS), lambda i, plan_ref, rot_ref: (i, 0, 0)),
            ],
        )
        return pl.pallas_call(
            functools.partial(maps_kernel, step, per),
            grid_spec=grid_spec,
            out_shape=[
                (pltpu.VMEM if UP_PERMUTE[s] else pltpu.HBM)((group, per, 2, HS, HS), F32),
                pltpu.HBM((heads, rows, 2 * HS), BF16),
            ],
            cost_estimate=cost(heads * 6 * rows * 256 * 256, heads * rows * HS * 12),
            compiler_params=limit(SMALL),
        )(plan, rots[UP_PERMUTE[s]], in_hbm(keys), in_hbm(values), in_hbm(token_gate), head_rate)

    def reads_of(s, errors):
        return pl.pallas_call(
            functools.partial(reads_kernel, step),
            grid_spec=pltpu.PrefetchScalarGridSpec(
                num_scalar_prefetch=1,
                grid=(heads // step,),
                in_specs=[seq_block(s), seq_block(s), gate_block(s), smem, t_block],
                out_specs=[col_block, col_block],
            ),
            out_shape=[
                pltpu.HBM((rows, width), BF16),
                pltpu.HBM((rows, width), F32),
            ],
            cost_estimate=cost(heads * 8 * rows * 256 * 256, heads * rows * HS * 16),
            compiler_params=limit(SMALL),
        )(plan, in_hbm(queries), in_hbm(keys), in_hbm(token_gate), head_rate, in_hbm(errors))

    def one_of(parts_d, blocks):
        tail = (0,) * (len(blocks) - 1)
        if isinstance(parts_d, list):
            return parts_d, [pl.BlockSpec(blocks, lambda i, *_: (0,) + tail) for _ in parts_d]
        return [parts_d] * group, [pl.BlockSpec(blocks, lambda i, *_, d=d: (d,) + tail) for d in range(group)]

    def chain(s, gathered, moved, all_out):
        shape = (group, per, HS, HS) if all_out else (per, HS, HS)
        info = jnp.concatenate([rots[UP_PERMUTE[s]], block.reshape(1), place.reshape(1), rots[DOWN_PERMUTE[s]]])
        given, map_specs = one_of(gathered, (1, per, 2, HS, HS))
        hops = moved is not None
        return pl.pallas_call(
            functools.partial(chain_kernel, group, hops, all_out),
            grid_spec=pltpu.PrefetchScalarGridSpec(
                num_scalar_prefetch=1,
                grid=(1,),
                in_specs=map_specs
                + [
                    pl.BlockSpec((per, HS, HS), lambda i, info_ref: (info_ref[2], 0, 0)),
                    pl.BlockSpec((per, HS, HS), lambda i, info_ref: (0, 0, 0)),
                ],
                out_specs=pl.BlockSpec(shape, lambda i, info_ref: (0,) * len(shape)),
                scratch_shapes=[pltpu.VMEM((group, per, 2, HS, HS), F32)],
            ),
            out_shape=(pltpu.HBM if all_out and not DOWN_PERMUTE[s] else pltpu.VMEM)(shape, F32),
            compiler_params=limit(SMALL),
            cost_estimate=cost(group * per * 6 * HS**3, group * per * HS * HS * 12),
        )(info, *map(in_vmem, given), in_hbm(init_state), in_vmem(moved) if hops else in_hbm(init_state))

    wide = WIDE if model % WIDE == 0 else model
    steps = heads // step

    def final_of(s, reads, entering):
        less, rest = reads
        piece = rows // parts
        early = lambda i: jnp.minimum(i, steps - 1)
        late = lambda i: jnp.maximum(i - steps, 0)
        by_cols = pl.BlockSpec((rows, step * HS), lambda i, *_: (0, early(i)))
        given, state_specs = one_of(entering, (1, per, HS, HS))
        return pl.pallas_call(
            functools.partial(final_kernel, steps, parts, group),
            grid_spec=pltpu.PrefetchScalarGridSpec(
                num_scalar_prefetch=3,
                grid=(steps + model // wide,),
                in_specs=[
                    pl.BlockSpec((1, rows, step * HS), lambda i, plan_ref, *_: (plan_ref[s], 0, early(i))),
                    by_cols,
                    by_cols,
                    pl.BlockSpec((1, step * HS), lambda i, *_: (0, early(i))),
                    pl.BlockSpec(memory_space=pltpu.HBM),
                ]
                + state_specs,
                out_specs=[pl.BlockSpec((piece, wide), lambda i, *_: (0, late(i)))] * parts,
                scratch_shapes=[
                    pltpu.VMEM((group, per, HS, HS), F32),
                    pltpu.VMEM((steps, rows, step * HS), BF16),
                    pltpu.VMEM((model // wide, steps, step * HS, wide), BF16),
                    pltpu.SemaphoreType.DMA((model // wide,)),
                ],
            ),
            compiler_params=limit(LARGE),
            out_shape=[jax.ShapeDtypeStruct((piece, model), F32)] * parts,
            cost_estimate=cost(2 * rows * width * model, 2 * width * model + 4 * rows * model),
        )(
            plan,
            me,
            rots[DOWN_PERMUTE[s]],
            in_hbm(queries),
            in_hbm(less),
            in_hbm(rest),
            in_hbm(norm_gain.reshape(1, width)),
            in_hbm(out_proj.reshape(steps, step * HS, model)),
            *map(in_vmem, given),
        )

    def shared(pieces, permute):
        if group == 1:
            return pieces
        if not permute:
            return lax.all_to_all(pieces, "ctx", 0, 0, tiled=True, axis_index_groups=groups)
        outs = [pieces[:1]]
        for d in range(1, group):
            outs.append(lax.ppermute(pieces[d : d + 1], "ctx", [(i, i ^ d) for i in range(ctx)]))
        return outs

    mapped = [maps_of(s) for s in range(seqs)]
    gathered = [shared(maps, UP_PERMUTE[s]) for s, (maps, _) in enumerate(mapped)]
    reads = [reads_of(s, errors) for s, (_, errors) in enumerate(mapped)]
    gathered[0], reads = lax.optimization_barrier((gathered[0], reads))
    outs = []
    for s in range(seqs):
        moved = None
        for _ in range(ctx // group - 1):
            ending = chain(s, gathered[s], moved, False)
            moved = lax.ppermute(ending, "ctx", onward)
        leaving = chain(s, gathered[s], moved, True)
        entering = shared(leaving, DOWN_PERMUTE[s])
        products = final_of(s, reads[s], entering)
        total = products[0]
        for d in range(1, parts):
            other = lax.ppermute(products[d], "head", [(i, i ^ d) for i in range(parts)])
            total = total + other
        outs.append(total)
    return jnp.stack(outs, axis=1).astype(BF16)


def solution(mesh):
    return jax.shard_map(
        per_device,
        mesh=mesh,
        in_specs=(
            P(None, "ctx", "head"),
            P(None, "ctx", "head"),
            P(None, "ctx", "head"),
            P(None, "head", "ctx"),
            P("head"),
            P("head", None, None),
            P("head"),
            P("head", None),
            P(),
        ),
        out_specs=P(("ctx", "head"), None, None),
        check_vma=False,
    )
```

profile of v0, /device:TPU:0, one launch (start us, length us, event | category | flops | bytes accessed | tf_op | source)
XLA Modules:
  0.0 141.2 jit_solution(1465510057314458268)
XLA Ops:
  0.0 5.9 %shard_map.91 = (f32[8,2,2,128,128]{4,3,2,1,0:T(8,128)}, bf16[16,256,256]{2,1,0:T(8,128)(2,1)}) custom-call(s32[2]{0:T(128)} %plan_ref.11, s32[1]{0:T(128)} %constant.13.clone.1.rot_ref, bf16[2,256,2048]{2,1,0:T(8,128)(2,1)} %k_ref.7, bf16[2,256,2048]{2,1,0:T(8,128)(2,1)} %v_ref.3, f32[2,16,256]{2,1,0:T(8,128)} %gate_ref.7, f32[16]{0:T(128)} %rate_ref.7), custom_call_target="tpu_custom_call" | custom-call | flops 1610612736 | bytes 6291456 | tf_op jit(solution)/shard_map/pallas_call | solution.py:226
  5.9 6.2 %all-to-all-start = ((f32[8,2,2,128,128]{4,3,2,1,0:T(8,128)}), f32[8,2,2,128,128]{4,3,2,1,0:T(8,128)S(1)}, u32[]{:S(2)}, u32[]{:S(2)}) async-start(f32[8,2,2,128,128]{4,3,2,1,0:T(8,128)} %get-tuple-element.22), calls=%async_computation | async-start | bytes 4194304 | tf_op jit(solution)/shard_map/all_to_all | solution.py:333
  12.1 5.4 %shard_map.93 = (f32[8,2,2,128,128]{4,3,2,1,0:T(8,128)S(1)}, bf16[16,256,256]{2,1,0:T(8,128)(2,1)}) custom-call(s32[2]{0:T(128)} %plan_ref.11, s32[1]{0:T(128)} %bitcast.1.rot_ref, bf16[2,256,2048]{2,1,0:T(8,128)(2,1)} %k_ref.7, bf16[2,256,2048]{2,1,0:T(8,128)(2,1)} %v_ref.3, f32[2,16,256]{2,1,0:T(8,128)} %gate_ref.7, f32[16]{0:T(128)} %rate_ref.7), custom_call_target="tpu_custom_call" | custom-call | flops 1610612736 | bytes 6291456 | tf_op jit(solution)/shard_map/pallas_call | solution.py:226
  17.4 1.3 fusion.2
  18.7 3.8 %collective-permute-start.8 = (f32[1,2,2,128,128]{4,3,2,1,0:T(8,128)}, f32[1,2,2,128,128]{4,3,2,1,0:T(8,128)S(1)}, u32[]{:S(2)}, u32[]{:S(2)}) collective-permute-start(f32[1,2,2,128,128]{4,3,2,1,0:T(8,128)} %get-tuple-element.39), channel_id=1, source_target_pairs={{0,14},{2,12},{4,10},{6,8},{8,6},{10,4},{12,2},{14,0},{16,30},{18,... | collective-permute-start | bytes 786440 | tf_op jit(solution)/shard_map/ppermute | solution.py:336
  22.6 0.6 collective-permute-start.7
  23.1 5.0 %shard_map.94 = (bf16[256,2048]{1,0:T(8,128)(2,1)}, f32[256,2048]{1,0:T(8,128)}) custom-call(s32[2]{0:T(128)} %plan_ref.11, bf16[2,256,2048]{2,1,0:T(8,128)(2,1)} %q_ref.7, bf16[2,256,2048]{2,1,0:T(8,128)(2,1)} %k_ref.7, f32[2,16,256]{2,1,0:T(8,128)} %gate_ref.7, f32[16]{0:T(128)} %rate_ref.7, bf16[16,256,256]{2,1,0:T(8,128)(2,1)} %get-tuple-element.26.t_ref), custom_call_target="tpu_custom_call" | custom-call | flops 2147483648 | bytes 8388608 | tf_op jit(solution)/shard_map/pallas_call | solution.py:238
  28.1 5.0 %shard_map.92 = (bf16[256,2048]{1,0:T(8,128)(2,1)}, f32[256,2048]{1,0:T(8,128)}) custom-call(s32[2]{0:T(128)} %plan_ref.11, bf16[2,256,2048]{2,1,0:T(8,128)(2,1)} %q_ref.7, bf16[2,256,2048]{2,1,0:T(8,128)(2,1)} %k_ref.7, f32[2,16,256]{2,1,0:T(8,128)} %gate_ref.7, f32[16]{0:T(128)} %rate_ref.7, bf16[16,256,256]{2,1,0:T(8,128)(2,1)} %get-tuple-element.23.t_ref), custom_call_target="tpu_custom_call" | custom-call | flops 2147483648 | bytes 8388608 | tf_op jit(solution)/shard_map/pallas_call | solution.py:238
  33.1 0.1 pad_add_fusion.info_ref
  33.1 8.7 %all-to-all-done.refs_0_.refs_1_.refs_2_.refs_3_.refs_4_.refs_5_.refs_6_.refs_7_ = f32[8,2,2,128,128]{4,3,2,1,0:T(8,128)S(1)} async-done(((f32[8,2,2,128,128]{4,3,2,1,0:T(8,128)}), f32[8,2,2,128,128]{4,3,2,1,0:T(8,128)S(1)}, u32[]{:S(2)}, u32[]{:S(2)}) %all-to-all-start) | async-done | bytes 2097184 | tf_op jit(solution)/shard_map/all_to_all | solution.py:333
  41.8 2.8 %shard_map.95 = f32[2,128,128]{2,1,0:T(8,128)S(1)} custom-call(s32[4]{0:T(128)S(1)} %pad_add_fusion.info_ref, f32[8,2,2,128,128]{4,3,2,1,0:T(8,128)S(1)} %all-to-all-done.refs_0_.refs_1_.refs_2_.refs_3_.refs_4_.refs_5_.refs_6_.refs_7_, f32[8,2,2,128,128]{4,3,2,1,0:T(8,128)S(1)} %all-to-all-done.refs_0_.refs_1_.refs_2_.refs_3_.refs_4_.refs_5_.refs_6_.refs_7_, ...), custom_call_target="tpu_custom_call" | custom-call | flops 201326592 | bytes 3145728 | tf_op jit(solution)/shard_map/pallas_call | solution.py:265
  44.6 4.5 %collective-permute-start = (f32[2,128,128]{2,1,0:T(8,128)S(1)}, f32[2,128,128]{2,1,0:T(8,128)S(1)}, u32[]{:S(2)}, u32[]{:S(2)}) collective-permute-start(f32[2,128,128]{2,1,0:T(8,128)S(1)} %shard_map.95), channel_id=1, source_target_pairs={{0,16},{2,18},{4,20},{6,22},{8,24},{10,26},{12,28},{14,30},{1,17},... | collective-permute-start | bytes 393224 | tf_op jit(solution)/shard_map/ppermute | solution.py:348
  49.1 4.1 %collective-permute-start.6 = (f32[1,2,2,128,128]{4,3,2,1,0:T(8,128)}, f32[1,2,2,128,128]{4,3,2,1,0:T(8,128)S(1)}, u32[]{:S(2)}, u32[]{:S(2)}) collective-permute-start(f32[1,2,2,128,128]{4,3,2,1,0:T(8,128)} %get-tuple-element.41), channel_id=1, source_target_pairs={{0,10},{2,8},{4,14},{6,12},{8,2},{10,0},{12,6},{14,4},{16,26},{18,... | collective-permute-start | bytes 786440 | tf_op jit(solution)/shard_map/ppermute | solution.py:336
  53.2 0.0 collective-permute-start.5
  53.2 0.0 collective-permute-done.8.refs_7_
  53.2 1.8 %collective-permute-start.4 = (f32[1,2,2,128,128]{4,3,2,1,0:T(8,128)}, f32[1,2,2,128,128]{4,3,2,1,0:T(8,128)}, u32[]{:S(2)}, u32[]{:S(2)}) collective-permute-start(f32[1,2,2,128,128]{4,3,2,1,0:T(8,128)} %get-tuple-element.43), channel_id=1, source_target_pairs={{0,6},{2,4},{4,2},{6,0},{8,14},{10,12},{12,10},{14,8},{16,22},{18,... | collective-permute-start | bytes 786440 | tf_op jit(solution)/shard_map/ppermute | solution.py:336
  55.0 0.0 collective-permute-done.7.refs_6_
  55.0 0.3 collective-permute-start.3
  55.3 0.0 collective-permute-done.refs_9_
  55.3 1.4 %collective-permute-start.2 = (f32[1,2,2,128,128]{4,3,2,1,0:T(8,128)}, f32[1,2,2,128,128]{4,3,2,1,0:T(8,128)}, u32[]{:S(2)}, u32[]{:S(2)}) collective-permute-start(f32[1,2,2,128,128]{4,3,2,1,0:T(8,128)} %get-tuple-element.45), channel_id=1, source_target_pairs={{0,2},{2,0},{4,6},{6,4},{8,10},{10,8},{12,14},{14,12},{16,18},{18,... | collective-permute-start | bytes 786440 | tf_op jit(solution)/shard_map/ppermute | solution.py:336
  56.7 3.6 %shard_map.96 = f32[8,2,128,128]{3,2,1,0:T(8,128)} custom-call(s32[4]{0:T(128)S(1)} %pad_add_fusion.info_ref, f32[8,2,2,128,128]{4,3,2,1,0:T(8,128)S(1)} %all-to-all-done.refs_0_.refs_1_.refs_2_.refs_3_.refs_4_.refs_5_.refs_6_.refs_7_, f32[8,2,2,128,128]{4,3,2,1,0:T(8,128)S(1)} %all-to-all-done.refs_0_.refs_1_.refs_2_.refs_3_.refs_4_.refs_5_.refs_6_.refs_7_, ...), custom_call_target="tpu_custom_call" | custom-call | flops 201326592 | bytes 3145728 | tf_op jit(solution)/shard_map/pallas_call | solution.py:265
  60.4 4.4 %all-to-all-start.1 = ((f32[8,2,128,128]{3,2,1,0:T(8,128)}), f32[8,2,128,128]{3,2,1,0:T(8,128)S(1)}, u32[]{:S(2)}, u32[]{:S(2)}) async-start(f32[8,2,128,128]{3,2,1,0:T(8,128)} %shard_map.96), calls=%async_computation.1 | async-start | bytes 2097152 | tf_op jit(solution)/shard_map/all_to_all | solution.py:333
  64.8 0.1 pad_add_fusion.1.info_ref
  64.9 0.0 collective-permute-done.6.refs_5_
  64.9 0.9 collective-permute-done.5.refs_4_
  65.8 0.9 collective-permute-done.4.refs_3_
  66.6 5.1 %collective-permute-done.3.refs_2_ = f32[1,2,2,128,128]{4,3,2,1,0:T(8,128)} collective-permute-done((f32[1,2,2,128,128]{4,3,2,1,0:T(8,128)}, f32[1,2,2,128,128]{4,3,2,1,0:T(8,128)}, u32[]{:S(2)}, u32[]{:S(2)}) %collective-permute-start.3) | collective-permute-done | bytes 262176 | tf_op jit(solution)/shard_map/ppermute | solution.py:336
  71.7 5.0 %collective-permute-done.2.refs_1_ = f32[1,2,2,128,128]{4,3,2,1,0:T(8,128)} collective-permute-done((f32[1,2,2,128,128]{4,3,2,1,0:T(8,128)}, f32[1,2,2,128,128]{4,3,2,1,0:T(8,128)}, u32[]{:S(2)}, u32[]{:S(2)}) %collective-permute-start.2) | collective-permute-done | bytes 262176 | tf_op jit(solution)/shard_map/ppermute | solution.py:336
  76.7 3.0 %shard_map.98 = f32[2,128,128]{2,1,0:T(8,128)S(1)} custom-call(s32[4]{0:T(128)S(1)} %pad_add_fusion.1.info_ref, f32[1,2,2,128,128]{4,3,2,1,0:T(8,128)S(1)} %get-tuple-element.46.refs_0_, f32[1,2,2,128,128]{4,3,2,1,0:T(8,128)} %collective-permute-done.2.refs_1_, f32[1,2,2,128,128]{4,3,2,1,0:T(8,128)} %collective-permute-done.3.refs_2_, ...), custom_call_target="tpu_custom_call" | custom-call | flops 201326592 | bytes 3145728 | tf_op jit(solution)/shard_map/pallas_call | solution.py:265
  79.8 1.5 %collective-permute-start.9 = (f32[2,128,128]{2,1,0:T(8,128)S(1)}, f32[2,128,128]{2,1,0:T(8,128)S(1)}, u32[]{:S(2)}, u32[]{:S(2)}) collective-permute-start(f32[2,128,128]{2,1,0:T(8,128)S(1)} %shard_map.98), channel_id=1, source_target_pairs={{0,16},{2,18},{4,20},{6,22},{8,24},{10,26},{12,28},{14,30},{1,17},... | collective-permute-start | bytes 393224 | tf_op jit(solution)/shard_map/ppermute | solution.py:348
  81.2 2.3 %collective-permute-done.9.refs_9_ = f32[2,128,128]{2,1,0:T(8,128)S(1)} collective-permute-done((f32[2,128,128]{2,1,0:T(8,128)S(1)}, f32[2,128,128]{2,1,0:T(8,128)S(1)}, u32[]{:S(2)}, u32[]{:S(2)}) %collective-permute-start.9) | collective-permute-done | bytes 131104 | tf_op jit(solution)/shard_map/ppermute | solution.py:348
  83.6 2.8 %shard_map.99 = f32[8,2,128,128]{3,2,1,0:T(8,128)S(1)} custom-call(s32[4]{0:T(128)S(1)} %pad_add_fusion.1.info_ref, f32[1,2,2,128,128]{4,3,2,1,0:T(8,128)S(1)} %get-tuple-element.46.refs_0_, f32[1,2,2,128,128]{4,3,2,1,0:T(8,128)} %collective-permute-done.2.refs_1_, f32[1,2,2,128,128]{4,3,2,1,0:T(8,128)} %collective-permute-done.3.refs_2_, ...), custom_call_target="tpu_custom_call" | custom-call | flops 201326592 | bytes 3145728 | tf_op jit(solution)/shard_map/pallas_call | solution.py:265
  86.4 0.1 fusion.3
  86.5 4.9 %collective-permute-start.16 = (f32[1,2,128,128]{3,2,1,0:T(8,128)S(1)}, f32[1,2,128,128]{3,2,1,0:T(8,128)S(1)}, u32[]{:S(2)}, u32[]{:S(2)}) collective-permute-start(f32[1,2,128,128]{3,2,1,0:T(8,128)S(1)} %get-tuple-element.47), channel_id=1, source_target_pairs={{0,14},{2,12},{4,10},{6,8},{8,6},{10,4},{12,2},{14,0},{16,30},{18,... | collective-permute-start | bytes 393224 | tf_op jit(solution)/shard_map/ppermute | solution.py:336
  91.3 1.2 collective-permute-start.15
  92.5 1.9 %collective-permute-start.14 = (f32[1,2,128,128]{3,2,1,0:T(8,128)S(1)}, f32[1,2,128,128]{3,2,1,0:T(8,128)S(1)}, u32[]{:S(2)}, u32[]{:S(2)}) collective-permute-start(f32[1,2,128,128]{3,2,1,0:T(8,128)S(1)} %get-tuple-element.49), channel_id=1, source_target_pairs={{0,10},{2,8},{4,14},{6,12},{8,2},{10,0},{12,6},{14,4},{16,26},{18,... | collective-permute-start | bytes 393224 | tf_op jit(solution)/shard_map/ppermute | solution.py:336
  94.4 1.0 collective-permute-start.13
  95.4 1.5 %collective-permute-start.12 = (f32[1,2,128,128]{3,2,1,0:T(8,128)S(1)}, f32[1,2,128,128]{3,2,1,0:T(8,128)S(1)}, u32[]{:S(2)}, u32[]{:S(2)}) collective-permute-start(f32[1,2,128,128]{3,2,1,0:T(8,128)S(1)} %get-tuple-element.51), channel_id=1, source_target_pairs={{0,6},{2,4},{4,2},{6,0},{8,14},{10,12},{12,10},{14,8},{16,22},{18,... | collective-permute-start | bytes 393224 | tf_op jit(solution)/shard_map/ppermute | solution.py:336
  96.8 0.0 collective-permute-done.16.refs_7_
  96.8 0.6 collective-permute-start.11
  97.5 2.4 %collective-permute-done.15.refs_6_ = f32[1,2,128,128]{3,2,1,0:T(8,128)S(1)} collective-permute-done((f32[1,2,128,128]{3,2,1,0:T(8,128)S(1)}, f32[1,2,128,128]{3,2,1,0:T(8,128)S(1)}, u32[]{:S(2)}, u32[]{:S(2)}) %collective-permute-start.15) | collective-permute-done | bytes 131104 | tf_op jit(solution)/shard_map/ppermute | solution.py:336
  99.9 2.2 %collective-permute-start.10 = (f32[1,2,128,128]{3,2,1,0:T(8,128)S(1)}, f32[1,2,128,128]{3,2,1,0:T(8,128)S(1)}, u32[]{:S(2)}, u32[]{:S(2)}) collective-permute-start(f32[1,2,128,128]{3,2,1,0:T(8,128)S(1)} %get-tuple-element.53), channel_id=1, source_target_pairs={{0,2},{2,0},{4,6},{6,4},{8,10},{10,8},{12,14},{14,12},{16,18},{18,... | collective-permute-start | bytes 393224 | tf_op jit(solution)/shard_map/ppermute | solution.py:336
  102.1 0.0 collective-permute-done.14.refs_5_
  102.1 0.6 copy-done
  102.7 0.6 copy-done.2
  103.4 1.3 collective-permute-done.12.refs_3_
  104.6 0.7 copy-done.4
  105.3 0.7 copy-done.6
  105.9 0.7 copy-done.8
  106.6 0.9 copy-done.1
  107.5 0.9 copy-done.3
  108.4 0.9 copy-done.5
  109.3 0.9 copy-done.7
  110.2 0.9 copy-done.9
  111.1 11.1 %shard_map.100 = (f32[128,4096]{1,0:T(8,128)S(1)}, f32[128,4096]{1,0:T(8,128)}) custom-call(s32[2]{0:T(128)} %plan_ref.11, s32[1]{0:T(128)} %bitcast.me_ref, s32[1]{0:T(128)} %bitcast.1.rot_ref, bf16[2,256,2048]{2,1,0:T(8,128)(2,1)} %q_ref.7, bf16[256,2048]{1,0:T(8,128)(2,1)} %get-tuple-element.34.less_ref, f32[256,2048]{1,0:T(8,128)} %get-tuple-element.35.rest_ref, ...), custom_call_target="tpu_custom_call" | custom-call | flops 4294967296 | bytes 20971520 | tf_op jit(solution)/shard_map/pallas_call | solution.py:293
  122.3 0.1 collective-permute-start.17
  122.3 10.5 %shard_map.97 = (f32[128,4096]{1,0:T(8,128)S(1)}, f32[128,4096]{1,0:T(8,128)S(1)}) custom-call(s32[2]{0:T(128)} %plan_ref.11, s32[1]{0:T(128)} %bitcast.me_ref, s32[1]{0:T(128)} %constant.13.clone.1.rot_ref, bf16[2,256,2048]{2,1,0:T(8,128)(2,1)} %q_ref.7, bf16[256,2048]{1,0:T(8,128)(2,1)} %get-tuple-element.29.less_ref, ...), custom_call_target="tpu_custom_call" | custom-call | flops 4294967296 | bytes 20971520 | tf_op jit(solution)/shard_map/pallas_call | solution.py:293
  132.9 0.5 collective-permute-start.1
  133.4 0.0 collective-permute-done.17
  133.4 1.8 %fusion.1 = bf16[128,1,4096]{2,0,1:T(8,128)(2,1)S(1)} fusion(f32[128,4096]{1,0:T(8,128)S(1)} %get-tuple-element.37, f32[128,4096]{1,0:T(8,128)} %collective-permute-done.17), kind=kLoop, calls=%fused_computation.4 | loop fusion | flops 1048576 | bytes 5242880 | tf_op jit(solution)/shard_map/stack | solution.py:357
  135.2 2.0 %collective-permute-done.1 = f32[128,4096]{1,0:T(8,128)S(1)} collective-permute-done((f32[128,4096]{1,0:T(8,128)S(1)}, f32[128,4096]{1,0:T(8,128)S(1)}, u32[]{:S(2)}, u32[]{:S(2)}) %collective-permute-start.1) | collective-permute-done | bytes 2097184 | tf_op jit(solution)/shard_map/ppermute | solution.py:354
  137.2 0.3 fusion
  137.5 0.2 pad_maximum_fusion
  137.7 3.5 %copy.10 = bf16[128,2,4096]{2,1,0:T(2,128)(2,1)} copy(bf16[128,2,4096]{2,0,1:T(8,128)(2,1)S(1)} %pad_maximum_fusion) | data formatting | bytes 4194304 | tf_op jit(solution)/shard_map/stack | solution.py:357
  (14 shorter events, 0.0 us)
Async XLA Ops:
  5.9 35.9 %all-to-all-start = ((f32[8,2,2,128,128]{4,3,2,1,0:T(8,128)}), f32[8,2,2,128,128]{4,3,2,1,0:T(8,128)S(1)}, u32[]{:S(2)}, u32[]{:S(2)}) async-start(f32[8,2,2,128,128]{4,3,2,1,0:T(8,128)} %get-tuple-element.22), calls=%async_computation | async-start | bytes 4194304 | tf_op jit(solution)/shard_map/all_to_all | solution.py:333
  18.7 34.5 %collective-permute-start.8 = (f32[1,2,2,128,128]{4,3,2,1,0:T(8,128)}, f32[1,2,2,128,128]{4,3,2,1,0:T(8,128)S(1)}, u32[]{:S(2)}, u32[]{:S(2)}) collective-permute-start(f32[1,2,2,128,128]{4,3,2,1,0:T(8,128)} %get-tuple-element.39), channel_id=1, source_target_pairs={{0,14},{2,12},{4,10},{6,8},{8,6},{10,4},{12,2},{14,0},{16,30},{18,... | collective-permute-start | bytes 786440 | tf_op jit(solution)/shard_map/ppermute | solution.py:336
  22.6 32.5 %collective-permute-start.7 = (f32[1,2,2,128,128]{4,3,2,1,0:T(8,128)}, f32[1,2,2,128,128]{4,3,2,1,0:T(8,128)S(1)}, u32[]{:S(2)}, u32[]{:S(2)}) collective-permute-start(f32[1,2,2,128,128]{4,3,2,1,0:T(8,128)} %get-tuple-element.40), channel_id=1, source_target_pairs={{0,12},{2,14},{4,8},{6,10},{8,4},{10,6},{12,0},{14,2},{16,28},{18,... | collective-permute-start | bytes 786440 | tf_op jit(solution)/shard_map/ppermute | solution.py:336
  44.6 10.7 %collective-permute-start = (f32[2,128,128]{2,1,0:T(8,128)S(1)}, f32[2,128,128]{2,1,0:T(8,128)S(1)}, u32[]{:S(2)}, u32[]{:S(2)}) collective-permute-start(f32[2,128,128]{2,1,0:T(8,128)S(1)} %shard_map.95), channel_id=1, source_target_pairs={{0,16},{2,18},{4,20},{6,22},{8,24},{10,26},{12,28},{14,30},{1,17},... | collective-permute-start | bytes 393224 | tf_op jit(solution)/shard_map/ppermute | solution.py:348
  49.1 15.7 %collective-permute-start.6 = (f32[1,2,2,128,128]{4,3,2,1,0:T(8,128)}, f32[1,2,2,128,128]{4,3,2,1,0:T(8,128)S(1)}, u32[]{:S(2)}, u32[]{:S(2)}) collective-permute-start(f32[1,2,2,128,128]{4,3,2,1,0:T(8,128)} %get-tuple-element.41), channel_id=1, source_target_pairs={{0,10},{2,8},{4,14},{6,12},{8,2},{10,0},{12,6},{14,4},{16,26},{18,... | collective-permute-start | bytes 786440 | tf_op jit(solution)/shard_map/ppermute | solution.py:336
  53.2 12.6 %collective-permute-start.5 = (f32[1,2,2,128,128]{4,3,2,1,0:T(8,128)}, f32[1,2,2,128,128]{4,3,2,1,0:T(8,128)S(1)}, u32[]{:S(2)}, u32[]{:S(2)}) collective-permute-start(f32[1,2,2,128,128]{4,3,2,1,0:T(8,128)} %get-tuple-element.42), channel_id=1, source_target_pairs={{0,8},{2,10},{4,12},{6,14},{8,0},{10,2},{12,4},{14,6},{16,24},{18,... | collective-permute-start | bytes 786440 | tf_op jit(solution)/shard_map/ppermute | solution.py:336
  53.2 13.4 %collective-permute-start.4 = (f32[1,2,2,128,128]{4,3,2,1,0:T(8,128)}, f32[1,2,2,128,128]{4,3,2,1,0:T(8,128)}, u32[]{:S(2)}, u32[]{:S(2)}) collective-permute-start(f32[1,2,2,128,128]{4,3,2,1,0:T(8,128)} %get-tuple-element.43), channel_id=1, source_target_pairs={{0,6},{2,4},{4,2},{6,0},{8,14},{10,12},{12,10},{14,8},{16,22},{18,... | collective-permute-start | bytes 786440 | tf_op jit(solution)/shard_map/ppermute | solution.py:336
  55.0 16.7 %collective-permute-start.3 = (f32[1,2,2,128,128]{4,3,2,1,0:T(8,128)}, f32[1,2,2,128,128]{4,3,2,1,0:T(8,128)}, u32[]{:S(2)}, u32[]{:S(2)}) collective-permute-start(f32[1,2,2,128,128]{4,3,2,1,0:T(8,128)} %get-tuple-element.44), channel_id=1, source_target_pairs={{0,4},{2,6},{4,0},{6,2},{8,12},{10,14},{12,8},{14,10},{16,20},{18,... | collective-permute-start | bytes 786440 | tf_op jit(solution)/shard_map/ppermute | solution.py:336
  55.3 21.4 %collective-permute-start.2 = (f32[1,2,2,128,128]{4,3,2,1,0:T(8,128)}, f32[1,2,2,128,128]{4,3,2,1,0:T(8,128)}, u32[]{:S(2)}, u32[]{:S(2)}) collective-permute-start(f32[1,2,2,128,128]{4,3,2,1,0:T(8,128)} %get-tuple-element.45), channel_id=1, source_target_pairs={{0,2},{2,0},{4,6},{6,4},{8,10},{10,8},{12,14},{14,12},{16,18},{18,... | collective-permute-start | bytes 786440 | tf_op jit(solution)/shard_map/ppermute | solution.py:336
  60.4 62.0 %all-to-all-start.1 = ((f32[8,2,128,128]{3,2,1,0:T(8,128)}), f32[8,2,128,128]{3,2,1,0:T(8,128)S(1)}, u32[]{:S(2)}, u32[]{:S(2)}) async-start(f32[8,2,128,128]{3,2,1,0:T(8,128)} %shard_map.96), calls=%async_computation.1 | async-start | bytes 2097152 | tf_op jit(solution)/shard_map/all_to_all | solution.py:333
  79.8 3.8 %collective-permute-start.9 = (f32[2,128,128]{2,1,0:T(8,128)S(1)}, f32[2,128,128]{2,1,0:T(8,128)S(1)}, u32[]{:S(2)}, u32[]{:S(2)}) collective-permute-start(f32[2,128,128]{2,1,0:T(8,128)S(1)} %shard_map.98), channel_id=1, source_target_pairs={{0,16},{2,18},{4,20},{6,22},{8,24},{10,26},{12,28},{14,30},{1,17},... | collective-permute-start | bytes 393224 | tf_op jit(solution)/shard_map/ppermute | solution.py:348
  86.5 10.3 %collective-permute-start.16 = (f32[1,2,128,128]{3,2,1,0:T(8,128)S(1)}, f32[1,2,128,128]{3,2,1,0:T(8,128)S(1)}, u32[]{:S(2)}, u32[]{:S(2)}) collective-permute-start(f32[1,2,128,128]{3,2,1,0:T(8,128)S(1)} %get-tuple-element.47), channel_id=1, source_target_pairs={{0,14},{2,12},{4,10},{6,8},{8,6},{10,4},{12,2},{14,0},{16,30},{18,... | collective-permute-start | bytes 393224 | tf_op jit(solution)/shard_map/ppermute | solution.py:336
  91.3 8.5 %collective-permute-start.15 = (f32[1,2,128,128]{3,2,1,0:T(8,128)S(1)}, f32[1,2,128,128]{3,2,1,0:T(8,128)S(1)}, u32[]{:S(2)}, u32[]{:S(2)}) collective-permute-start(f32[1,2,128,128]{3,2,1,0:T(8,128)S(1)} %get-tuple-element.48), channel_id=1, source_target_pairs={{0,12},{2,14},{4,8},{6,10},{8,4},{10,6},{12,0},{14,2},{16,28},{18,... | collective-permute-start | bytes 393224 | tf_op jit(solution)/shard_map/ppermute | solution.py:336
  92.5 9.6 %collective-permute-start.14 = (f32[1,2,128,128]{3,2,1,0:T(8,128)S(1)}, f32[1,2,128,128]{3,2,1,0:T(8,128)S(1)}, u32[]{:S(2)}, u32[]{:S(2)}) collective-permute-start(f32[1,2,128,128]{3,2,1,0:T(8,128)S(1)} %get-tuple-element.49), channel_id=1, source_target_pairs={{0,10},{2,8},{4,14},{6,12},{8,2},{10,0},{12,6},{14,4},{16,26},{18,... | collective-permute-start | bytes 393224 | tf_op jit(solution)/shard_map/ppermute | solution.py:336
  94.4 8.3 %collective-permute-start.13 = (f32[1,2,128,128]{3,2,1,0:T(8,128)S(1)}, f32[1,2,128,128]{3,2,1,0:T(8,128)S(1)}, u32[]{:S(2)}, u32[]{:S(2)}) collective-permute-start(f32[1,2,128,128]{3,2,1,0:T(8,128)S(1)} %get-tuple-element.50), channel_id=1, source_target_pairs={{0,8},{2,10},{4,12},{6,14},{8,0},{10,2},{12,4},{14,6},{16,24},{18,... | collective-permute-start | bytes 393224 | tf_op jit(solution)/shard_map/ppermute | solution.py:336
  95.4 9.3 %collective-permute-start.12 = (f32[1,2,128,128]{3,2,1,0:T(8,128)S(1)}, f32[1,2,128,128]{3,2,1,0:T(8,128)S(1)}, u32[]{:S(2)}, u32[]{:S(2)}) collective-permute-start(f32[1,2,128,128]{3,2,1,0:T(8,128)S(1)} %get-tuple-element.51), channel_id=1, source_target_pairs={{0,6},{2,4},{4,2},{6,0},{8,14},{10,12},{12,10},{14,8},{16,22},{18,... | collective-permute-start | bytes 393224 | tf_op jit(solution)/shard_map/ppermute | solution.py:336
  96.8 8.5 %collective-permute-start.11 = (f32[1,2,128,128]{3,2,1,0:T(8,128)S(1)}, f32[1,2,128,128]{3,2,1,0:T(8,128)S(1)}, u32[]{:S(2)}, u32[]{:S(2)}) collective-permute-start(f32[1,2,128,128]{3,2,1,0:T(8,128)S(1)} %get-tuple-element.52), channel_id=1, source_target_pairs={{0,4},{2,6},{4,0},{6,2},{8,12},{10,14},{12,8},{14,10},{16,20},{18,... | collective-permute-start | bytes 393224 | tf_op jit(solution)/shard_map/ppermute | solution.py:336
  99.9 6.1 %collective-permute-start.10 = (f32[1,2,128,128]{3,2,1,0:T(8,128)S(1)}, f32[1,2,128,128]{3,2,1,0:T(8,128)S(1)}, u32[]{:S(2)}, u32[]{:S(2)}) collective-permute-start(f32[1,2,128,128]{3,2,1,0:T(8,128)S(1)} %get-tuple-element.53), channel_id=1, source_target_pairs={{0,2},{2,0},{4,6},{6,4},{8,10},{10,8},{12,14},{14,12},{16,18},{18,... | collective-permute-start | bytes 393224 | tf_op jit(solution)/shard_map/ppermute | solution.py:336
  102.1 0.6 copy-start
  102.7 0.7 copy-start.2
  104.6 0.7 copy-start.4
  105.3 0.7 copy-start.6
  105.9 0.7 copy-start.8
  106.6 0.9 copy-start.1
  107.5 0.9 copy-start.3
  108.4 0.9 copy-start.5
  109.3 0.9 copy-start.7
  110.2 0.9 copy-start.9
  122.3 11.1 %collective-permute-start.17 = (f32[128,4096]{1,0:T(8,128)}, f32[128,4096]{1,0:T(8,128)}, u32[]{:S(2)}, u32[]{:S(2)}) collective-permute-start(f32[128,4096]{1,0:T(8,128)} %get-tuple-element.38), channel_id=1, source_target_pairs={{0,1},{1,0},{2,3},{3,2},{4,5},{5,4},{6,7},{7,6},{8,9},{9,8},{10,11... | collective-permute-start | bytes 6291464 | tf_op jit(solution)/shard_map/ppermute | solution.py:354
  132.9 4.3 %collective-permute-start.1 = (f32[128,4096]{1,0:T(8,128)S(1)}, f32[128,4096]{1,0:T(8,128)S(1)}, u32[]{:S(2)}, u32[]{:S(2)}) collective-permute-start(f32[128,4096]{1,0:T(8,128)S(1)} %get-tuple-element.33), channel_id=1, source_target_pairs={{0,1},{1,0},{2,3},{3,2},{4,5},{5,4},{6,7},{7,6},{8,9},{9,8},{10,11... | collective-permute-start | bytes 6291464 | tf_op jit(solution)/shard_map/ppermute | solution.py:354
where the time goes:
time: 143 us; the launch traced here: 141 us
  Pallas kernels  55.1 us (39%)
  starting transfers between devices  42.4 us (30%)
  waiting for transfers between devices  28.6 us (20%)
  local copies, waits for them, and re-layouts  12.7 us (9%)
  other arithmetic  2.43 us (2%)
    ppermute x14, starting transfers between devices, shared(): lax.ppermute(pieces[d:d + 1], 'ctx', [(i, i ^ d) for i in range(ctx)])  25.1 us
    pallas_call x2, Pallas kernels, final_of(): pl.pallas_call(functools.partial(final_kernel, steps, parts, group), grid...  21.6 us
    ppermute x14, waiting for transfers between devices, shared(): lax.ppermute(pieces[d:d + 1], 'ctx', [(i, i ^ d) for i in range(ctx)])  15.6 us
    pallas_call x4, Pallas kernels, chain(): pl.pallas_call(functools.partial(chain_kernel, group, hops, all_out), gri...  12.3 us
    pallas_call x2, Pallas kernels, maps_of(): pl.pallas_call(functools.partial(maps_kernel, step, per), grid_spec=grid_...  11.2 us
    all_to_all x2, starting transfers between devices, shared(): lax.all_to_all(pieces, 'ctx', 0, 0, tiled=True, axis_index_groups=groups)  10.6 us
    pallas_call x2, Pallas kernels, reads_of(): pl.pallas_call(functools.partial(reads_kernel, step), grid_spec=pltpu.Pre...  9.94 us
    all_to_all x2, waiting for transfers between devices, shared(): lax.all_to_all(pieces, 'ctx', 0, 0, tiled=True, axis_index_groups=groups)  8.67 us
  transfers between devices with their start and end apart: 20, of which 9 were waited for; matrix products, arithmetic and copies ran while one was open for 2% of the time, Pallas kernels for 35%

commit v1 on v0

--- a/solution.py
+++ b/solution.py
@@ -16,7 +16,7 @@
 SMALL = 14
 LARGE = 30
 UP_PERMUTE = (False, True)
-DOWN_PERMUTE = (False, True)
+DOWN_PERMUTE = (False, False)
 F32 = jnp.float32
 BF16 = jnp.bfloat16
 
@@ -86,28 +86,41 @@
             cols = slice(h * HS, (h + 1) * HS)
             taken = mm(scores[h], t_ref[h, :end])
             less_ref[begin:end, cols] = taken[:, :HS].astype(BF16)
-            rest_ref[begin:end, cols] = taken[:, HS:]
+            rest_ref[begin:end, cols] = taken[:, HS:].astype(BF16)
 
 
 def advance(state, both):
     return state - mm(both[0].astype(BF16), state.astype(BF16)) - both[1]
 
 
-def chain_kernel(group, hops, all_out, info_ref, *refs):
-    maps, (start_ref, moved_ref), out_ref, held = refs[:group], refs[group:-2], refs[-2], refs[-1]
-    rot = info_ref[0]
-    for d in range(group):
-        held[d ^ rot] = maps[d][0]
-    per = held.shape[1]
+def chain_kernel(group, hops, all_out, one, streamed, info_ref, start_ref, *refs):
+    moved_ref, refs = (refs[0], refs[1:]) if hops else (None, refs)
+    count = 1 if one else group
+    maps, out_ref, held = refs[:count], refs[count], refs[count + 1 :]
+    copies = []
+    if streamed:
+        far_ref, out_ref, sems = out_ref, held[-2], held[-1]
+        copies = [pltpu.make_async_copy(out_ref.at[m], far_ref.at[m], sems.at[m]) for m in range(group)]
+    if one:
+        source = maps[0]
+    else:
+        source = held[0]
+        for d in range(group):
+            source[d ^ info_ref[0]] = maps[d][0]
+    per = source.shape[1]
     states = [start_ref[u] for u in range(per)]
     if hops:
         states = [jnp.where(info_ref[1] == 0, states[u], moved_ref[u]) for u in range(per)]
     for m in range(group):
         for u in range(per):
             if all_out:
-                out_ref[m ^ info_ref[3], u] = states[u]
+                out_ref[m if streamed else m ^ info_ref[2], u] = states[u]
             if not all_out or m < group - 1:
-                states[u] = advance(states[u], held[m, u])
+                states[u] = advance(states[u], source[m, u])
+        if streamed:
+            copies[m].start()
+    for copy in copies:
+        copy.wait()
     if not all_out:
         for u in range(per):
             out_ref[u] = states[u]
@@ -143,7 +156,7 @@
             small = (state - main.astype(F32)).astype(BF16)
             q = q_ref[0, :, cols]
             z = mm(jnp.concatenate([q, less_ref[:, cols]], axis=1), jnp.concatenate([main, main], axis=0))
-            zs.append(z + mm(q, small) + rest_ref[:, cols])
+            zs.append(z + mm(q, small) + rest_ref[:, cols].astype(F32))
         for h in range(heads_step):
             cols = slice(h * HS, (h + 1) * HS)
             scale = lax.rsqrt(jnp.mean(zs[h] * zs[h], axis=-1, keepdims=True) + EPS)
@@ -158,6 +171,16 @@
         product = sum(mm(normed[n], proj[i - steps, n]) for n in range(steps))
         for d in range(parts):
             outs[d][...] = product[d * piece : (d + 1) * piece]
+
+
+def sum_kernel(parts, *refs):
+    seqs = len(refs[:-1]) // parts
+    sums = [sum(ref[...] for ref in refs[s * parts : (s + 1) * parts]) for s in range(seqs)]
+    rows = jnp.concatenate(sums, axis=0).astype(BF16)
+    count, each = rows.shape[0], sums[0].shape[0]
+    to, of = iotas(count, count)
+    pick = jnp.where(lax.rem(to, seqs) * each + lax.div(to, seqs) == of, 1.0, 0.0).astype(BF16)
+    refs[-1][...] = mm(pick, rows).astype(BF16).reshape(each, seqs, rows.shape[1])
 
 
 def in_hbm(x):
@@ -245,7 +268,7 @@
             ),
             out_shape=[
                 pltpu.HBM((rows, width), BF16),
-                pltpu.HBM((rows, width), F32),
+                pltpu.HBM((rows, width), BF16),
             ],
             cost_estimate=cost(heads * 8 * rows * 256 * 256, heads * rows * HS * 16),
             compiler_params=limit(SMALL),
@@ -257,28 +280,28 @@
             return parts_d, [pl.BlockSpec(blocks, lambda i, *_: (0,) + tail) for _ in parts_d]
         return [parts_d] * group, [pl.BlockSpec(blocks, lambda i, *_, d=d: (d,) + tail) for d in range(group)]
 
+    start = lax.dynamic_slice_in_dim(init_state, place * per, per)
+
     def chain(s, gathered, moved, all_out):
         shape = (group, per, HS, HS) if all_out else (per, HS, HS)
-        info = jnp.concatenate([rots[UP_PERMUTE[s]], block.reshape(1), place.reshape(1), rots[DOWN_PERMUTE[s]]])
-        given, map_specs = one_of(gathered, (1, per, 2, HS, HS))
+        info = jnp.concatenate([rots[UP_PERMUTE[s]], block.reshape(1), rots[DOWN_PERMUTE[s]]])
+        one = not isinstance(gathered, list)
         hops = moved is not None
+        given = ([start, moved] if hops else [start]) + ([gathered] if one else gathered)
+        vmem = pl.BlockSpec(memory_space=pltpu.VMEM)
+        streamed = all_out and not DOWN_PERMUTE[s]
+        scratch = [] if one else [pltpu.VMEM((group, per, 2, HS, HS), F32)]
+        if streamed:
+            scratch += [pltpu.VMEM(shape, F32), pltpu.SemaphoreType.DMA((group,))]
         return pl.pallas_call(
-            functools.partial(chain_kernel, group, hops, all_out),
-            grid_spec=pltpu.PrefetchScalarGridSpec(
-                num_scalar_prefetch=1,
-                grid=(1,),
-                in_specs=map_specs
-                + [
-                    pl.BlockSpec((per, HS, HS), lambda i, info_ref: (info_ref[2], 0, 0)),
-                    pl.BlockSpec((per, HS, HS), lambda i, info_ref: (0, 0, 0)),
-                ],
-                out_specs=pl.BlockSpec(shape, lambda i, info_ref: (0,) * len(shape)),
-                scratch_shapes=[pltpu.VMEM((group, per, 2, HS, HS), F32)],
-            ),
-            out_shape=(pltpu.HBM if all_out and not DOWN_PERMUTE[s] else pltpu.VMEM)(shape, F32),
+            functools.partial(chain_kernel, group, hops, all_out, one, streamed),
+            in_specs=[smem] + [vmem] * len(given),
+            out_specs=pl.BlockSpec(memory_space=pltpu.HBM) if streamed else vmem,
+            scratch_shapes=scratch,
+            out_shape=pltpu.HBM(shape, F32) if streamed else jax.ShapeDtypeStruct(shape, F32),
             compiler_params=limit(SMALL),
             cost_estimate=cost(group * per * 6 * HS**3, group * per * HS * HS * 12),
-        )(info, *map(in_vmem, given), in_hbm(init_state), in_vmem(moved) if hops else in_hbm(init_state))
+        )(info, *map(in_vmem, given))
 
     wide = WIDE if model % WIDE == 0 else model
     steps = heads // step
@@ -349,12 +372,21 @@
         leaving = chain(s, gathered[s], moved, True)
         entering = shared(leaving, DOWN_PERMUTE[s])
         products = final_of(s, reads[s], entering)
-        total = products[0]
+        outs.append(products[0])
         for d in range(1, parts):
-            other = lax.ppermute(products[d], "head", [(i, i ^ d) for i in range(parts)])
-            total = total + other
-        outs.append(total)
-    return jnp.stack(outs, axis=1).astype(BF16)
+            outs.append(lax.ppermute(products[d], "head", [(i, i ^ d) for i in range(parts)]))
+    piece = rows // parts
+    wider = 2048 if model % 2048 == 0 else model
+    return pl.pallas_call(
+        functools.partial(sum_kernel, parts),
+        grid=(model // wider,),
+        in_specs=[pl.BlockSpec((piece, wider), lambda i: (0, i))] * len(outs),
+        out_specs=pl.BlockSpec((piece, seqs, wider), lambda i: (0, 0, i)),
+        out_shape=jax.ShapeDtypeStruct((piece, seqs, model), BF16),
+        compiler_params=limit(2 * SMALL),
+        cost_estimate=cost(2 * (piece * seqs) ** 2 * model, 4 * len(outs) * piece * model),
+        name="sums",
+    )(*outs)
 
 
 def solution(mesh):

time: 143 us -> 149 us (1.042); the launches traced: 141 us -> 149 us
  waiting for transfers between devices: 28.6 us -> 44.8 us
  local copies, waits for them, and re-layouts: 12.7 us -> 7.1 us
  other arithmetic: 2.43 us -> 0.15 us
    ppermute x14 -> x7, waiting for transfers between devices: 15.6 us -> 33.9 us  [shared(): lax.ppermute(pieces[d:d + 1], 'ctx', [(i, i ^ d) for i in range(ctx)])]
    ppermute x14 -> x7, starting transfers between devices: 25.1 us -> 12.7 us  [shared(): lax.ppermute(pieces[d:d + 1], 'ctx', [(i, i ^ d) for i in range(ctx)])]
    all_to_all x2 -> x3, starting transfers between devices: 10.6 us -> 18.7 us  [shared(): lax.all_to_all(pieces, 'ctx', 0, 0, tiled=True, axis_index_groups=groups)]
    all_to_all x2 -> x3, waiting for transfers between devices: 8.67 us -> 1.67 us  [shared(): lax.all_to_all(pieces, 'ctx', 0, 0, tiled=True, axis_index_groups=groups)]
    ppermute x2, starting transfers between devices: 5.99 us -> 9.79 us  [per_device(): moved = lax.ppermute(ending, 'ctx', onward)]
    another operation x1 -> x0, local copies, waits for them, and re-layouts: 3.52 us -> none  [per_device(): return jnp.stack(outs, axis=1).astype(BF16)]
    ppermute x2, waiting for transfers between devices: 2.33 us -> 5.04 us  [per_device(): moved = lax.ppermute(ending, 'ctx', onward)]
    another operation x3 -> x0, other arithmetic: 2.28 us -> none  [per_device(): return jnp.stack(outs, axis=1).astype(BF16)]
  transfers between devices with their start and end apart: 20 -> 14, of which waited for: 9 -> 9; matrix products, arithmetic and copies ran while one was open for 2% -> 1% of each run, Pallas kernels for 35% -> 31%
where the time goes in v1:
time: 149 us
  Pallas kernels  55.4 us (37%)
  waiting for transfers between devices  44.8 us (30%)
  starting transfers between devices  41.3 us (28%)
  local copies, waits for them, and re-layouts  7.1 us (5%)
    ppermute x7, waiting for transfers between devices, shared(): lax.ppermute(pieces[d:d + 1], 'ctx', [(i, i ^ d) for i in range(ctx)])  33.9 us
    pallas_call x2, Pallas kernels, final_of(): pl.pallas_call(functools.partial(final_kernel, steps, parts, group), grid...  21.4 us
    all_to_all x3, starting transfers between devices, shared(): lax.all_to_all(pieces, 'ctx', 0, 0, tiled=True, axis_index_groups=groups)  18.7 us
    ppermute x7, starting transfers between devices, shared(): lax.ppermute(pieces[d:d + 1], 'ctx', [(i, i ^ d) for i in range(ctx)])  12.7 us
    pallas_call x2, Pallas kernels, maps_of(): pl.pallas_call(functools.partial(maps_kernel, step, per), grid_spec=grid_...  11.3 us
    ppermute x2, starting transfers between devices, per_device(): moved = lax.ppermute(ending, 'ctx', onward)  9.79 us
    pallas_call x4, Pallas kernels, chain(): pl.pallas_call(functools.partial(chain_kernel, group, hops, all_out, one,...  9.71 us
    pallas_call x2, Pallas kernels, reads_of(): pl.pallas_call(functools.partial(reads_kernel, step), grid_spec=pltpu.Pre...  9.7 us
  transfers between devices with their start and end apart: 14, of which 9 were waited for; matrix products, arithmetic and copies ran while one was open for 1% of the time, Pallas kernels for 31%

profile of v1, /device:TPU:0, one launch (start us, length us, event | category | flops | bytes accessed | tf_op | source)
XLA Modules:
  0.0 148.8 jit_solution(10506543272855792247)
XLA Ops:
  0.0 0.0 copy-start
  0.0 5.9 %shard_map.91 = (f32[8,2,2,128,128]{4,3,2,1,0:T(8,128)}, bf16[16,256,256]{2,1,0:T(8,128)(2,1)}) custom-call(s32[2]{0:T(128)} %plan_ref.11, s32[1]{0:T(128)} %constant.16.clone.1.rot_ref, bf16[2,256,2048]{2,1,0:T(8,128)(2,1)} %k_ref.7, bf16[2,256,2048]{2,1,0:T(8,128)(2,1)} %v_ref.3, f32[2,16,256]{2,1,0:T(8,128)} %gate_ref.7, f32[16]{0:T(128)} %rate_ref.7), custom_call_target="tpu_custom_call" | custom-call | flops 1610612736 | bytes 6291456 | tf_op jit(solution)/shard_map/pallas_call | solution.py:249
  5.9 6.2 %all-to-all-start = ((f32[8,2,2,128,128]{4,3,2,1,0:T(8,128)}), f32[8,2,2,128,128]{4,3,2,1,0:T(8,128)S(1)}, u32[]{:S(2)}, u32[]{:S(2)}) async-start(f32[8,2,2,128,128]{4,3,2,1,0:T(8,128)} %get-tuple-element.22), calls=%async_computation | async-start | bytes 4194304 | tf_op jit(solution)/shard_map/all_to_all | solution.py:356
  12.2 5.4 %shard_map.93 = (f32[8,2,2,128,128]{4,3,2,1,0:T(8,128)S(1)}, bf16[16,256,256]{2,1,0:T(8,128)(2,1)}) custom-call(s32[2]{0:T(128)} %plan_ref.11, s32[1]{0:T(128)} %bitcast.1.rot_ref, bf16[2,256,2048]{2,1,0:T(8,128)(2,1)} %k_ref.7, bf16[2,256,2048]{2,1,0:T(8,128)(2,1)} %v_ref.3, f32[2,16,256]{2,1,0:T(8,128)} %gate_ref.7, f32[16]{0:T(128)} %rate_ref.7), custom_call_target="tpu_custom_call" | custom-call | flops 1610612736 | bytes 6291456 | tf_op jit(solution)/shard_map/pallas_call | solution.py:249
  17.5 1.1 fusion
  18.7 3.8 %collective-permute-start.8 = (f32[1,2,2,128,128]{4,3,2,1,0:T(8,128)S(1)}, f32[1,2,2,128,128]{4,3,2,1,0:T(8,128)S(1)}, u32[]{:S(2)}, u32[]{:S(2)}) collective-permute-start(f32[1,2,2,128,128]{4,3,2,1,0:T(8,128)S(1)} %get-tuple-element.39), channel_id=1, source_target_pairs={{0,14},{2,12},{4,10},{6,8},{8,6},{10,4},{12,2},{14,0},{16,30},{18,... | collective-permute-start | bytes 786440 | tf_op jit(solution)/shard_map/ppermute | solution.py:359
  22.5 0.6 collective-permute-start.7
  23.1 1.5 collective-permute-start.6
  24.5 0.0 collective-permute-start.5
  24.5 2.9 %collective-permute-start.4 = (f32[1,2,2,128,128]{4,3,2,1,0:T(8,128)}, f32[1,2,2,128,128]{4,3,2,1,0:T(8,128)}, u32[]{:S(2)}, u32[]{:S(2)}) collective-permute-start(f32[1,2,2,128,128]{4,3,2,1,0:T(8,128)} %get-tuple-element.43), channel_id=1, source_target_pairs={{0,6},{2,4},{4,2},{6,0},{8,14},{10,12},{12,10},{14,8},{16,22},{18,... | collective-permute-start | bytes 786440 | tf_op jit(solution)/shard_map/ppermute | solution.py:359
  27.5 23.4 %collective-permute-done.8.refs_7_.refs_8_ = f32[1,2,2,128,128]{4,3,2,1,0:T(8,128)S(1)} collective-permute-done((f32[1,2,2,128,128]{4,3,2,1,0:T(8,128)S(1)}, f32[1,2,2,128,128]{4,3,2,1,0:T(8,128)S(1)}, u32[]{:S(2)}, u32[]{:S(2)}) %collective-permute-start.8) | collective-permute-done | bytes 262176 | tf_op jit(solution)/shard_map/ppermute | solution.py:359
  50.9 0.0 copy-start.5
  50.9 0.7 copy-done.5
  51.6 0.6 collective-permute-start.3
  52.1 2.8 %collective-permute-done.7.refs_6_.refs_7_ = f32[1,2,2,128,128]{4,3,2,1,0:T(8,128)S(1)} collective-permute-done((f32[1,2,2,128,128]{4,3,2,1,0:T(8,128)S(1)}, f32[1,2,2,128,128]{4,3,2,1,0:T(8,128)S(1)}, u32[]{:S(2)}, u32[]{:S(2)}) %collective-permute-start.7) | collective-permute-done | bytes 262176 | tf_op jit(solution)/shard_map/ppermute | solution.py:359
  54.9 0.0 copy-start.7
  54.9 0.7 copy-done.7
  55.6 3.3 %collective-permute-start.2 = (f32[1,2,2,128,128]{4,3,2,1,0:T(8,128)}, f32[1,2,2,128,128]{4,3,2,1,0:T(8,128)}, u32[]{:S(2)}, u32[]{:S(2)}) collective-permute-start(f32[1,2,2,128,128]{4,3,2,1,0:T(8,128)} %get-tuple-element.45), channel_id=1, source_target_pairs={{0,2},{2,0},{4,6},{6,4},{8,10},{10,8},{12,14},{14,12},{16,18},{18,... | collective-permute-start | bytes 786440 | tf_op jit(solution)/shard_map/ppermute | solution.py:359
  58.9 0.1 pad_add_fusion.info_ref
  59.0 0.0 copy-done
  59.0 3.5 %collective-permute-done.6.refs_5_.refs_6_ = f32[1,2,2,128,128]{4,3,2,1,0:T(8,128)} collective-permute-done((f32[1,2,2,128,128]{4,3,2,1,0:T(8,128)}, f32[1,2,2,128,128]{4,3,2,1,0:T(8,128)}, u32[]{:S(2)}, u32[]{:S(2)}) %collective-permute-start.6) | collective-permute-done | bytes 262176 | tf_op jit(solution)/shard_map/ppermute | solution.py:359
  62.6 0.4 collective-permute-done.5.refs_4_.refs_5_
  63.0 0.0 collective-permute-done.4.refs_3_.refs_4_
  63.0 0.0 collective-permute-done.3.refs_2_.refs_3_
  63.0 3.8 %collective-permute-done.2.refs_1_.refs_2_ = f32[1,2,2,128,128]{4,3,2,1,0:T(8,128)} collective-permute-done((f32[1,2,2,128,128]{4,3,2,1,0:T(8,128)}, f32[1,2,2,128,128]{4,3,2,1,0:T(8,128)}, u32[]{:S(2)}, u32[]{:S(2)}) %collective-permute-start.2) | collective-permute-done | bytes 262176 | tf_op jit(solution)/shard_map/ppermute | solution.py:359
  66.8 0.0 copy-start.6
  66.8 0.9 copy-done.6
  67.7 0.0 copy-start.8
  67.7 0.9 copy-done.8
  68.7 2.6 %shard_map.98 = f32[2,128,128]{2,1,0:T(8,128)S(1)} custom-call(s32[3]{0:T(128)S(1)} %pad_add_fusion.info_ref, f32[2,128,128]{2,1,0:T(8,128)S(1)} %constant_dynamic-slice_fusion.start_ref, f32[1,2,2,128,128]{4,3,2,1,0:T(8,128)S(1)} %get-tuple-element.46.refs_0_.refs_1_, f32[1,2,2,128,128]{4,3,2,1,0:T(8,128)} %collective-permute-done.2.refs_1_.refs_2_, ...), custom_call_target="tpu_custom_call" | custom-call | flops 201326592 | bytes 3145728 | tf_op jit(solution)/shard_map/pallas_call | solution.py:296
  71.2 4.5 %collective-permute-start.9 = (f32[2,128,128]{2,1,0:T(8,128)S(1)}, f32[2,128,128]{2,1,0:T(8,128)S(1)}, u32[]{:S(2)}, u32[]{:S(2)}) collective-permute-start(f32[2,128,128]{2,1,0:T(8,128)S(1)} %shard_map.98), channel_id=1, source_target_pairs={{0,16},{2,18},{4,20},{6,22},{8,24},{10,26},{12,28},{14,30},{1,17},... | collective-permute-start | bytes 393224 | tf_op jit(solution)/shard_map/ppermute | solution.py:371
  75.7 2.5 %collective-permute-done.9.refs_0_ = f32[2,128,128]{2,1,0:T(8,128)S(1)} collective-permute-done((f32[2,128,128]{2,1,0:T(8,128)S(1)}, f32[2,128,128]{2,1,0:T(8,128)S(1)}, u32[]{:S(2)}, u32[]{:S(2)}) %collective-permute-start.9) | collective-permute-done | bytes 131104 | tf_op jit(solution)/shard_map/ppermute | solution.py:371
  78.3 3.2 %shard_map.99 = f32[8,2,128,128]{3,2,1,0:T(8,128)} custom-call(s32[3]{0:T(128)S(1)} %pad_add_fusion.info_ref, f32[2,128,128]{2,1,0:T(8,128)S(1)} %constant_dynamic-slice_fusion.start_ref, f32[2,128,128]{2,1,0:T(8,128)S(1)} %collective-permute-done.9.refs_0_, f32[1,2,2,128,128]{4,3,2,1,0:T(8,128)S(1)} %get-tuple-element.46.refs_0_.refs_1_, ...), custom_call_target="tpu_custom_call" | custom-call | flops 201326592 | bytes 3145728 | tf_op jit(solution)/shard_map/pallas_call | solution.py:296
  81.4 0.0 all-to-all-done.refs_0_.refs_1_
  81.4 0.0 copy-start.1
  81.4 1.3 copy-done.1
  82.8 5.7 %all-to-all-start.2 = ((f32[8,2,128,128]{3,2,1,0:T(8,128)}), f32[8,2,128,128]{3,2,1,0:T(8,128)S(1)}, u32[]{:S(2)}, u32[]{:S(2)}) async-start(f32[8,2,128,128]{3,2,1,0:T(8,128)} %shard_map.99), calls=%async_computation.2 | async-start | bytes 2097152 | tf_op jit(solution)/shard_map/all_to_all | solution.py:356
  88.4 0.1 pad_add_fusion.1.info_ref
  88.5 4.8 %shard_map.94 = (bf16[256,2048]{1,0:T(8,128)(2,1)}, bf16[256,2048]{1,0:T(8,128)(2,1)}) custom-call(s32[2]{0:T(128)} %plan_ref.11, bf16[2,256,2048]{2,1,0:T(8,128)(2,1)} %q_ref.7, bf16[2,256,2048]{2,1,0:T(8,128)(2,1)} %k_ref.7, f32[2,16,256]{2,1,0:T(8,128)} %gate_ref.7, f32[16]{0:T(128)} %rate_ref.7, bf16[16,256,256]{2,1,0:T(8,128)(2,1)} %get-tuple-element.26.t_ref), custom_call_target="tpu_custom_call" | custom-call | flops 2147483648 | bytes 8388608 | tf_op jit(solution)/shard_map/pallas_call | solution.py:261
  93.3 0.0 copy-start.2
  93.3 4.9 %shard_map.92 = (bf16[256,2048]{1,0:T(8,128)(2,1)}, bf16[256,2048]{1,0:T(8,128)(2,1)}) custom-call(s32[2]{0:T(128)} %plan_ref.11, bf16[2,256,2048]{2,1,0:T(8,128)(2,1)} %q_ref.7, bf16[2,256,2048]{2,1,0:T(8,128)(2,1)} %k_ref.7, f32[2,16,256]{2,1,0:T(8,128)} %gate_ref.7, f32[16]{0:T(128)} %rate_ref.7, bf16[16,256,256]{2,1,0:T(8,128)(2,1)} %get-tuple-element.23.t_ref), custom_call_target="tpu_custom_call" | custom-call | flops 2147483648 | bytes 8388608 | tf_op jit(solution)/shard_map/pallas_call | solution.py:261
  98.2 0.0 copy-done.2
  98.2 1.7 %shard_map.95 = f32[2,128,128]{2,1,0:T(8,128)S(1)} custom-call(s32[3]{0:T(128)S(1)} %pad_add_fusion.1.info_ref, f32[2,128,128]{2,1,0:T(8,128)S(1)} %constant_dynamic-slice_fusion.start_ref, f32[8,2,2,128,128]{4,3,2,1,0:T(8,128)S(1)} %copy-done.2), custom_call_target="tpu_custom_call" | custom-call | flops 201326592 | bytes 3145728 | tf_op jit(solution)/shard_map/pallas_call | solution.py:296
  99.9 5.3 %collective-permute-start = (f32[2,128,128]{2,1,0:T(8,128)S(1)}, f32[2,128,128]{2,1,0:T(8,128)S(1)}, u32[]{:S(2)}, u32[]{:S(2)}) collective-permute-start(f32[2,128,128]{2,1,0:T(8,128)S(1)} %shard_map.95), channel_id=1, source_target_pairs={{0,16},{2,18},{4,20},{6,22},{8,24},{10,26},{12,28},{14,30},{1,17},... | collective-permute-start | bytes 393224 | tf_op jit(solution)/shard_map/ppermute | solution.py:371
  105.2 2.5 %collective-permute-done.refs_0_ = f32[2,128,128]{2,1,0:T(8,128)S(1)} collective-permute-done((f32[2,128,128]{2,1,0:T(8,128)S(1)}, f32[2,128,128]{2,1,0:T(8,128)S(1)}, u32[]{:S(2)}, u32[]{:S(2)}) %collective-permute-start) | collective-permute-done | bytes 131104 | tf_op jit(solution)/shard_map/ppermute | solution.py:371
  107.7 2.3 %shard_map.96 = f32[8,2,128,128]{3,2,1,0:T(8,128)} custom-call(s32[3]{0:T(128)S(1)} %pad_add_fusion.1.info_ref, f32[2,128,128]{2,1,0:T(8,128)S(1)} %constant_dynamic-slice_fusion.start_ref, f32[2,128,128]{2,1,0:T(8,128)S(1)} %collective-permute-done.refs_0_, f32[8,2,2,128,128]{4,3,2,1,0:T(8,128)S(1)} %copy-done.2), custom_call_target="tpu_custom_call" | custom-call | flops 201326592 | bytes 3145728 | tf_op jit(solution)/shard_map/pallas_call | solution.py:296
  110.0 0.0 all-to-all-done.2.refs_0_.refs_1_.refs_2_.refs_3_.refs_4_.refs_5_.refs_6_.refs_7_
  110.0 6.9 %all-to-all-start.1 = ((f32[8,2,128,128]{3,2,1,0:T(8,128)}), f32[8,2,128,128]{3,2,1,0:T(8,128)S(1)}, u32[]{:S(2)}, u32[]{:S(2)}) async-start(f32[8,2,128,128]{3,2,1,0:T(8,128)} %shard_map.96), calls=%async_computation.1 | async-start | bytes 2097152 | tf_op jit(solution)/shard_map/all_to_all | solution.py:356
  116.9 10.9 %shard_map.100 = (f32[128,4096]{1,0:T(8,128)S(1)}, f32[128,4096]{1,0:T(8,128)}) custom-call(s32[2]{0:T(128)} %plan_ref.11, s32[1]{0:T(128)} %bitcast.me_ref, s32[1]{0:T(128)} %constant.16.clone.1.rot_ref, bf16[2,256,2048]{2,1,0:T(8,128)(2,1)} %q_ref.7, bf16[256,2048]{1,0:T(8,128)(2,1)} %get-tuple-element.34.less_ref, ...), custom_call_target="tpu_custom_call" | custom-call | flops 4294967296 | bytes 20971520 | tf_op jit(solution)/shard_map/pallas_call | solution.py:316
  127.8 0.0 copy-start.3
  127.8 1.3 copy-done.3
  129.1 0.0 collective-permute-start.10
  129.1 1.7 %all-to-all-done.1.refs_0_.refs_1_.refs_2_.refs_3_.refs_4_.refs_5_.refs_6_.refs_7_ = f32[8,2,128,128]{3,2,1,0:T(8,128)S(1)} async-done(((f32[8,2,128,128]{3,2,1,0:T(8,128)}), f32[8,2,128,128]{3,2,1,0:T(8,128)S(1)}, u32[]{:S(2)}, u32[]{:S(2)}) %all-to-all-start.1) | async-done | bytes 1048608 | tf_op jit(solution)/shard_map/all_to_all | solution.py:356
  130.8 0.0 copy-start.4
  130.8 10.5 %shard_map.97 = (f32[128,4096]{1,0:T(8,128)S(1)}, f32[128,4096]{1,0:T(8,128)S(1)}) custom-call(s32[2]{0:T(128)} %plan_ref.11, s32[1]{0:T(128)} %bitcast.me_ref, s32[1]{0:T(128)} %constant.16.clone.1.rot_ref, bf16[2,256,2048]{2,1,0:T(8,128)(2,1)} %q_ref.7, bf16[256,2048]{1,0:T(8,128)(2,1)} %get-tuple-element.29.less_ref, ...), custom_call_target="tpu_custom_call" | custom-call | flops 4294967296 | bytes 20971520 | tf_op jit(solution)/shard_map/pallas_call | solution.py:316
  141.3 0.1 collective-permute-start.1
  141.3 0.0 collective-permute-done.10.refs_3_
  141.3 4.1 %collective-permute-done.1.refs_1_ = f32[128,4096]{1,0:T(8,128)S(1)} collective-permute-done((f32[128,4096]{1,0:T(8,128)S(1)}, f32[128,4096]{1,0:T(8,128)S(1)}, u32[]{:S(2)}, u32[]{:S(2)}) %collective-permute-start.1) | collective-permute-done | bytes 2097184 | tf_op jit(solution)/shard_map/ppermute | solution.py:377
  145.5 0.0 copy-done.4
  145.5 3.4 %sums.1 = bf16[128,2,4096]{2,1,0:T(2,128)(2,1)} custom-call(f32[128,4096]{1,0:T(8,128)S(1)} %get-tuple-element.32.refs_0_, f32[128,4096]{1,0:T(8,128)S(1)} %collective-permute-done.1.refs_1_, f32[128,4096]{1,0:T(8,128)S(1)} %copy-done.4, f32[128,4096]{1,0:T(8,128)} %collective-permute-done.10.refs_3_), custom_call_target="tpu_custom_call" | custom-call | flops 536870912 | bytes 8388608 | tf_op jit(solution)/shard_map/sums/pallas_call | solution.py:380
  (1 shorter events, 0.0 us)
Async XLA Ops:
  0.0 59.0 %copy-start = (f32[16,128,128]{2,1,0:T(8,128)S(1)}, f32[16,128,128]{2,1,0:T(8,128)}, u32[]{:S(2)}) copy-start(f32[16,128,128]{2,1,0:T(8,128)} %param.14) | copy-start | bytes 3145732
  5.9 75.5 %all-to-all-start = ((f32[8,2,2,128,128]{4,3,2,1,0:T(8,128)}), f32[8,2,2,128,128]{4,3,2,1,0:T(8,128)S(1)}, u32[]{:S(2)}, u32[]{:S(2)}) async-start(f32[8,2,2,128,128]{4,3,2,1,0:T(8,128)} %get-tuple-element.22), calls=%async_computation | async-start | bytes 4194304 | tf_op jit(solution)/shard_map/all_to_all | solution.py:356
  18.7 32.2 %collective-permute-start.8 = (f32[1,2,2,128,128]{4,3,2,1,0:T(8,128)S(1)}, f32[1,2,2,128,128]{4,3,2,1,0:T(8,128)S(1)}, u32[]{:S(2)}, u32[]{:S(2)}) collective-permute-start(f32[1,2,2,128,128]{4,3,2,1,0:T(8,128)S(1)} %get-tuple-element.39), channel_id=1, source_target_pairs={{0,14},{2,12},{4,10},{6,8},{8,6},{10,4},{12,2},{14,0},{16,30},{18,... | collective-permute-start | bytes 786440 | tf_op jit(solution)/shard_map/ppermute | solution.py:359
  22.5 32.4 %collective-permute-start.7 = (f32[1,2,2,128,128]{4,3,2,1,0:T(8,128)S(1)}, f32[1,2,2,128,128]{4,3,2,1,0:T(8,128)S(1)}, u32[]{:S(2)}, u32[]{:S(2)}) collective-permute-start(f32[1,2,2,128,128]{4,3,2,1,0:T(8,128)S(1)} %get-tuple-element.40), channel_id=1, source_target_pairs={{0,12},{2,14},{4,8},{6,10},{8,4},{10,6},{12,0},{14,2},{16,28},{18,... | collective-permute-start | bytes 786440 | tf_op jit(solution)/shard_map/ppermute | solution.py:359
  23.1 39.5 %collective-permute-start.6 = (f32[1,2,2,128,128]{4,3,2,1,0:T(8,128)}, f32[1,2,2,128,128]{4,3,2,1,0:T(8,128)}, u32[]{:S(2)}, u32[]{:S(2)}) collective-permute-start(f32[1,2,2,128,128]{4,3,2,1,0:T(8,128)} %get-tuple-element.41), channel_id=1, source_target_pairs={{0,10},{2,8},{4,14},{6,12},{8,2},{10,0},{12,6},{14,4},{16,26},{18,... | collective-permute-start | bytes 786440 | tf_op jit(solution)/shard_map/ppermute | solution.py:359
  24.5 38.5 %collective-permute-start.5 = (f32[1,2,2,128,128]{4,3,2,1,0:T(8,128)}, f32[1,2,2,128,128]{4,3,2,1,0:T(8,128)}, u32[]{:S(2)}, u32[]{:S(2)}) collective-permute-start(f32[1,2,2,128,128]{4,3,2,1,0:T(8,128)} %get-tuple-element.42), channel_id=1, source_target_pairs={{0,8},{2,10},{4,12},{6,14},{8,0},{10,2},{12,4},{14,6},{16,24},{18,... | collective-permute-start | bytes 786440 | tf_op jit(solution)/shard_map/ppermute | solution.py:359
  24.5 38.5 %collective-permute-start.4 = (f32[1,2,2,128,128]{4,3,2,1,0:T(8,128)}, f32[1,2,2,128,128]{4,3,2,1,0:T(8,128)}, u32[]{:S(2)}, u32[]{:S(2)}) collective-permute-start(f32[1,2,2,128,128]{4,3,2,1,0:T(8,128)} %get-tuple-element.43), channel_id=1, source_target_pairs={{0,6},{2,4},{4,2},{6,0},{8,14},{10,12},{12,10},{14,8},{16,22},{18,... | collective-permute-start | bytes 786440 | tf_op jit(solution)/shard_map/ppermute | solution.py:359
  50.9 0.7 copy-start.5
  51.6 11.5 %collective-permute-start.3 = (f32[1,2,2,128,128]{4,3,2,1,0:T(8,128)}, f32[1,2,2,128,128]{4,3,2,1,0:T(8,128)}, u32[]{:S(2)}, u32[]{:S(2)}) collective-permute-start(f32[1,2,2,128,128]{4,3,2,1,0:T(8,128)} %get-tuple-element.44), channel_id=1, source_target_pairs={{0,4},{2,6},{4,0},{6,2},{8,12},{10,14},{12,8},{14,10},{16,20},{18,... | collective-permute-start | bytes 786440 | tf_op jit(solution)/shard_map/ppermute | solution.py:359
  54.9 0.7 copy-start.7
  55.6 11.1 %collective-permute-start.2 = (f32[1,2,2,128,128]{4,3,2,1,0:T(8,128)}, f32[1,2,2,128,128]{4,3,2,1,0:T(8,128)}, u32[]{:S(2)}, u32[]{:S(2)}) collective-permute-start(f32[1,2,2,128,128]{4,3,2,1,0:T(8,128)} %get-tuple-element.45), channel_id=1, source_target_pairs={{0,2},{2,0},{4,6},{6,4},{8,10},{10,8},{12,14},{14,12},{16,18},{18,... | collective-permute-start | bytes 786440 | tf_op jit(solution)/shard_map/ppermute | solution.py:359
  66.8 1.0 copy-start.6
  67.7 0.9 copy-start.8
  71.2 7.0 %collective-permute-start.9 = (f32[2,128,128]{2,1,0:T(8,128)S(1)}, f32[2,128,128]{2,1,0:T(8,128)S(1)}, u32[]{:S(2)}, u32[]{:S(2)}) collective-permute-start(f32[2,128,128]{2,1,0:T(8,128)S(1)} %shard_map.98), channel_id=1, source_target_pairs={{0,16},{2,18},{4,20},{6,22},{8,24},{10,26},{12,28},{14,30},{1,17},... | collective-permute-start | bytes 393224 | tf_op jit(solution)/shard_map/ppermute | solution.py:371
  81.4 1.3 copy-start.1
  82.8 27.3 %all-to-all-start.2 = ((f32[8,2,128,128]{3,2,1,0:T(8,128)}), f32[8,2,128,128]{3,2,1,0:T(8,128)S(1)}, u32[]{:S(2)}, u32[]{:S(2)}) async-start(f32[8,2,128,128]{3,2,1,0:T(8,128)} %shard_map.99), calls=%async_computation.2 | async-start | bytes 2097152 | tf_op jit(solution)/shard_map/all_to_all | solution.py:356
  93.3 4.9 %copy-start.2 = (f32[8,2,2,128,128]{4,3,2,1,0:T(8,128)S(1)}, f32[8,2,2,128,128]{4,3,2,1,0:T(8,128)}, u32[]{:S(2)}) copy-start(f32[8,2,2,128,128]{4,3,2,1,0:T(8,128)} %copy-done.1) | copy-start | bytes 6291460
  99.9 7.8 %collective-permute-start = (f32[2,128,128]{2,1,0:T(8,128)S(1)}, f32[2,128,128]{2,1,0:T(8,128)S(1)}, u32[]{:S(2)}, u32[]{:S(2)}) collective-permute-start(f32[2,128,128]{2,1,0:T(8,128)S(1)} %shard_map.95), channel_id=1, source_target_pairs={{0,16},{2,18},{4,20},{6,22},{8,24},{10,26},{12,28},{14,30},{1,17},... | collective-permute-start | bytes 393224 | tf_op jit(solution)/shard_map/ppermute | solution.py:371
  110.0 20.8 %all-to-all-start.1 = ((f32[8,2,128,128]{3,2,1,0:T(8,128)}), f32[8,2,128,128]{3,2,1,0:T(8,128)S(1)}, u32[]{:S(2)}, u32[]{:S(2)}) async-start(f32[8,2,128,128]{3,2,1,0:T(8,128)} %shard_map.96), calls=%async_computation.1 | async-start | bytes 2097152 | tf_op jit(solution)/shard_map/all_to_all | solution.py:356
  127.8 1.3 copy-start.3
  129.1 12.2 %collective-permute-start.10 = (f32[128,4096]{1,0:T(8,128)}, f32[128,4096]{1,0:T(8,128)}, u32[]{:S(2)}, u32[]{:S(2)}) collective-permute-start(f32[128,4096]{1,0:T(8,128)} %get-tuple-element.38), channel_id=1, source_target_pairs={{0,1},{1,0},{2,3},{3,2},{4,5},{5,4},{6,7},{7,6},{8,9},{9,8},{10,11... | collective-permute-start | bytes 6291464 | tf_op jit(solution)/shard_map/ppermute | solution.py:377
  130.8 14.7 %copy-start.4 = (f32[128,4096]{1,0:T(8,128)S(1)}, f32[128,4096]{1,0:T(8,128)}, u32[]{:S(2)}) copy-start(f32[128,4096]{1,0:T(8,128)} %copy-done.3) | copy-start | bytes 6291460
  141.3 4.2 %collective-permute-start.1 = (f32[128,4096]{1,0:T(8,128)S(1)}, f32[128,4096]{1,0:T(8,128)S(1)}, u32[]{:S(2)}, u32[]{:S(2)}) collective-permute-start(f32[128,4096]{1,0:T(8,128)S(1)} %get-tuple-element.33), channel_id=1, source_target_pairs={{0,1},{1,0},{2,3},{3,2},{4,5},{5,4},{6,7},{7,6},{8,9},{9,8},{10,11... | collective-permute-start | bytes 6291464 | tf_op jit(solution)/shard_map/ppermute | solution.py:377

commit v2 on v1

--- a/solution.py
+++ b/solution.py
@@ -12,10 +12,10 @@
 MB = 64
 EPS = 1e-06
 STEP = 8
-WIDE = 512
+WIDE = 1024
 SMALL = 14
 LARGE = 30
-UP_PERMUTE = (False, True)
+UP_PERMUTE = (True, False)
 DOWN_PERMUTE = (False, False)
 F32 = jnp.float32
 BF16 = jnp.bfloat16
@@ -93,25 +93,31 @@
     return state - mm(both[0].astype(BF16), state.astype(BF16)) - both[1]
 
 
-def chain_kernel(group, hops, all_out, one, streamed, info_ref, start_ref, *refs):
+def chain_kernel(group, hops, all_out, kind, streamed, info_ref, start_ref, *refs):
     moved_ref, refs = (refs[0], refs[1:]) if hops else (None, refs)
-    count = 1 if one else group
-    maps, out_ref, held = refs[:count], refs[count], refs[count + 1 :]
-    copies = []
-    if streamed:
-        far_ref, out_ref, sems = out_ref, held[-2], held[-1]
-        copies = [pltpu.make_async_copy(out_ref.at[m], far_ref.at[m], sems.at[m]) for m in range(group)]
-    if one:
-        source = maps[0]
-    else:
-        source = held[0]
+    count = group if kind == "pieces" else 1
+    maps, out_ref, held = refs[:count], refs[count], list(refs[count + 1 :])
+    arrivals, copies = [], []
+    source = maps[0]
+    if kind == "pieces":
+        source = held.pop(0)
         for d in range(group):
             source[d ^ info_ref[0]] = maps[d][0]
+    elif kind == "far":
+        source, sems = held.pop(0), held.pop(0)
+        arrivals = [pltpu.make_async_copy(maps[0].at[m], source.at[m], sems.at[m]) for m in range(group)]
+        for arrival in arrivals:
+            arrival.start()
+    if streamed:
+        far_ref, out_ref, sems = out_ref, held[0], held[1]
+        copies = [pltpu.make_async_copy(out_ref.at[m], far_ref.at[m], sems.at[m]) for m in range(group)]
     per = source.shape[1]
     states = [start_ref[u] for u in range(per)]
     if hops:
         states = [jnp.where(info_ref[1] == 0, states[u], moved_ref[u]) for u in range(per)]
     for m in range(group):
+        if arrivals:
+            arrivals[m].wait()
         for u in range(per):
             if all_out:
                 out_ref[m if streamed else m ^ info_ref[2], u] = states[u]
@@ -148,15 +154,17 @@
     @pl.when(i < steps)
     def _():
         heads_step = normed.shape[2] // HS
+        none = jnp.zeros((HS, HS), BF16)
         zs = []
         for h in range(heads_step):
             cols = slice(h * HS, (h + 1) * HS)
             state = held[i * (heads_step // per) + h // per, h % per]
             main = state.astype(BF16)
             small = (state - main.astype(F32)).astype(BF16)
-            q = q_ref[0, :, cols]
-            z = mm(jnp.concatenate([q, less_ref[:, cols]], axis=1), jnp.concatenate([main, main], axis=0))
-            zs.append(z + mm(q, small) + rest_ref[:, cols].astype(F32))
+            left = jnp.concatenate([q_ref[0, :, cols], less_ref[:, cols]], axis=1)
+            top, bottom = jnp.concatenate([main, small], axis=1), jnp.concatenate([main, none], axis=1)
+            both = mm(left, jnp.concatenate([top, bottom], axis=0))
+            zs.append(both[:, :HS] + both[:, HS:] + rest_ref[:, cols].astype(F32))
         for h in range(heads_step):
             cols = slice(h * HS, (h + 1) * HS)
             scale = lax.rsqrt(jnp.mean(zs[h] * zs[h], axis=-1, keepdims=True) + EPS)
@@ -285,23 +293,30 @@
     def chain(s, gathered, moved, all_out):
         shape = (group, per, HS, HS) if all_out else (per, HS, HS)
         info = jnp.concatenate([rots[UP_PERMUTE[s]], block.reshape(1), rots[DOWN_PERMUTE[s]]])
-        one = not isinstance(gathered, list)
+        kind = "pieces" if isinstance(gathered, list) else "far" if s else "near"
         hops = moved is not None
-        given = ([start, moved] if hops else [start]) + ([gathered] if one else gathered)
-        vmem = pl.BlockSpec(memory_space=pltpu.VMEM)
+        given = [start, moved] if hops else [start]
+        vmem, hbm = pl.BlockSpec(memory_space=pltpu.VMEM), pl.BlockSpec(memory_space=pltpu.HBM)
+        given = [in_vmem(x) for x in given]
+        specs = [smem] + [vmem] * len(given)
+        pieces = gathered if kind == "pieces" else [gathered]
+        given += [in_hbm(x) if kind == "far" else in_vmem(x) for x in pieces]
+        specs += [hbm if kind == "far" else vmem] * len(pieces)
         streamed = all_out and not DOWN_PERMUTE[s]
-        scratch = [] if one else [pltpu.VMEM((group, per, 2, HS, HS), F32)]
+        scratch = [] if kind == "near" else [pltpu.VMEM((group, per, 2, HS, HS), F32)]
+        if kind == "far":
+            scratch.append(pltpu.SemaphoreType.DMA((group,)))
         if streamed:
             scratch += [pltpu.VMEM(shape, F32), pltpu.SemaphoreType.DMA((group,))]
         return pl.pallas_call(
-            functools.partial(chain_kernel, group, hops, all_out, one, streamed),
-            in_specs=[smem] + [vmem] * len(given),
-            out_specs=pl.BlockSpec(memory_space=pltpu.HBM) if streamed else vmem,
+            functools.partial(chain_kernel, group, hops, all_out, kind, streamed),
+            in_specs=specs,
+            out_specs=hbm if streamed else vmem,
             scratch_shapes=scratch,
             out_shape=pltpu.HBM(shape, F32) if streamed else jax.ShapeDtypeStruct(shape, F32),
             compiler_params=limit(SMALL),
             cost_estimate=cost(group * per * 6 * HS**3, group * per * HS * HS * 12),
-        )(info, *map(in_vmem, given))
+        )(info, *given)
 
     wide = WIDE if model % WIDE == 0 else model
     steps = heads // step
@@ -335,7 +350,7 @@
                 ],
             ),
             compiler_params=limit(LARGE),
-            out_shape=[jax.ShapeDtypeStruct((piece, model), F32)] * parts,
+            out_shape=[(pltpu.HBM if s < seqs - 1 else pltpu.VMEM)((piece, model), F32)] * parts,
             cost_estimate=cost(2 * rows * width * model, 2 * width * model + 4 * rows * model),
         )(
             plan,

time: 149 us -> 136 us (0.913)
  local copies, waits for them, and re-layouts: 7.1 us -> 1.1 us
  waiting for transfers between devices: 44.8 us -> 40.6 us
  starting transfers between devices: 41.3 us -> 37.4 us
    ppermute x7, waiting for transfers between devices: 33.9 us -> 25.6 us  [shared(): lax.ppermute(pieces[d:d + 1], 'ctx', [(i, i ^ d) for i in range(ctx)])]
    unnamed x18 -> x4, local copies, waits for them, and re-layouts: 5.94 us -> 0.01 us
    all_to_all x3, starting transfers between devices: 18.7 us -> 14.9 us  [shared(): lax.all_to_all(pieces, 'ctx', 0, 0, tiled=True, axis_index_groups=groups)]
    ppermute x2, waiting for transfers between devices: 5.04 us -> 8.68 us  [per_device(): moved = lax.ppermute(ending, 'ctx', onward)]
  transfers between devices with their start and end apart: 14 -> 14, of which waited for: 9 -> 7; matrix products, arithmetic and copies ran while one was open for 1% -> 1% of each run, Pallas kernels for 31% -> 34%
where the time goes in v2:
time: 136 us; the launch traced here: 135 us
  Pallas kernels  55.7 us (41%)
  waiting for transfers between devices  40.6 us (30%)
  starting transfers between devices  37.4 us (28%)
    ppermute x7, waiting for transfers between devices, shared(): lax.ppermute(pieces[d:d + 1], 'ctx', [(i, i ^ d) for i in range(ctx)])  25.6 us
    pallas_call x2, Pallas kernels, final_of(): pl.pallas_call(functools.partial(final_kernel, steps, parts, group), grid...  21.1 us
    all_to_all x3, starting transfers between devices, shared(): lax.all_to_all(pieces, 'ctx', 0, 0, tiled=True, axis_index_groups=groups)  14.9 us
    ppermute x7, starting transfers between devices, shared(): lax.ppermute(pieces[d:d + 1], 'ctx', [(i, i ^ d) for i in range(ctx)])  12.6 us
    pallas_call x2, Pallas kernels, maps_of(): pl.pallas_call(functools.partial(maps_kernel, step, per), grid_spec=grid_...  11.3 us
    pallas_call x4, Pallas kernels, chain(): pl.pallas_call(functools.partial(chain_kernel, group, hops, all_out, kind...  10.4 us
    ppermute x2, starting transfers between devices, per_device(): moved = lax.ppermute(ending, 'ctx', onward)  9.78 us
    pallas_call x2, Pallas kernels, reads_of(): pl.pallas_call(functools.partial(reads_kernel, step), grid_spec=pltpu.Pre...  9.71 us
  transfers between devices with their start and end apart: 14, of which 7 were waited for; matrix products, arithmetic and copies ran while one was open for 1% of the time, Pallas kernels for 34%

profile of v2, /device:TPU:0, one launch (start us, length us, event | category | flops | bytes accessed | tf_op | source)
XLA Modules:
  0.0 135.1 jit_solution(10738917247805585358)
XLA Ops:
  0.0 0.0 copy-start
  0.0 5.9 %shard_map.93 = (f32[8,2,2,128,128]{4,3,2,1,0:T(8,128)}, bf16[16,256,256]{2,1,0:T(8,128)(2,1)}) custom-call(s32[2]{0:T(128)} %plan_ref.11, s32[1]{0:T(128)} %constant.16.clone.1.rot_ref, bf16[2,256,2048]{2,1,0:T(8,128)(2,1)} %k_ref.7, bf16[2,256,2048]{2,1,0:T(8,128)(2,1)} %v_ref.3, f32[2,16,256]{2,1,0:T(8,128)} %gate_ref.7, f32[16]{0:T(128)} %rate_ref.7), custom_call_target="tpu_custom_call" | custom-call | flops 1610612736 | bytes 6291456 | tf_op jit(solution)/shard_map/pallas_call | solution.py:257
  5.9 6.2 %all-to-all-start.1 = ((f32[8,2,2,128,128]{4,3,2,1,0:T(8,128)}), f32[8,2,2,128,128]{4,3,2,1,0:T(8,128)}, u32[]{:S(2)}, u32[]{:S(2)}) async-start(f32[8,2,2,128,128]{4,3,2,1,0:T(8,128)} %get-tuple-element.50), calls=%async_computation.1 | async-start | bytes 4194304 | tf_op jit(solution)/shard_map/all_to_all | solution.py:371
  12.2 5.4 %shard_map.91 = (f32[8,2,2,128,128]{4,3,2,1,0:T(8,128)S(1)}, bf16[16,256,256]{2,1,0:T(8,128)(2,1)}) custom-call(s32[2]{0:T(128)} %plan_ref.11, s32[1]{0:T(128)} %bitcast.1.rot_ref, bf16[2,256,2048]{2,1,0:T(8,128)(2,1)} %k_ref.7, bf16[2,256,2048]{2,1,0:T(8,128)(2,1)} %v_ref.3, f32[2,16,256]{2,1,0:T(8,128)} %gate_ref.7, f32[16]{0:T(128)} %rate_ref.7), custom_call_target="tpu_custom_call" | custom-call | flops 1610612736 | bytes 6291456 | tf_op jit(solution)/shard_map/pallas_call | solution.py:257
  17.5 1.1 fusion
  18.6 3.8 %collective-permute-start.6 = (f32[1,2,2,128,128]{4,3,2,1,0:T(8,128)}, f32[1,2,2,128,128]{4,3,2,1,0:T(8,128)S(1)}, u32[]{:S(2)}, u32[]{:S(2)}) collective-permute-start(f32[1,2,2,128,128]{4,3,2,1,0:T(8,128)} %get-tuple-element.53), channel_id=1, source_target_pairs={{0,14},{2,12},{4,10},{6,8},{8,6},{10,4},{12,2},{14,0},{16,30},{18,... | collective-permute-start | bytes 786440 | tf_op jit(solution)/shard_map/ppermute | solution.py:374
  22.4 0.6 collective-permute-start.5
  23.0 1.5 %collective-permute-start.4 = (f32[1,2,2,128,128]{4,3,2,1,0:T(8,128)}, f32[1,2,2,128,128]{4,3,2,1,0:T(8,128)S(1)}, u32[]{:S(2)}, u32[]{:S(2)}) collective-permute-start(f32[1,2,2,128,128]{4,3,2,1,0:T(8,128)} %get-tuple-element.55), channel_id=1, source_target_pairs={{0,10},{2,8},{4,14},{6,12},{8,2},{10,0},{12,6},{14,4},{16,26},{18,... | collective-permute-start | bytes 786440 | tf_op jit(solution)/shard_map/ppermute | solution.py:374
  24.5 0.0 collective-permute-start.3
  24.5 2.9 %collective-permute-start.2 = (f32[1,2,2,128,128]{4,3,2,1,0:T(8,128)S(1)}, f32[1,2,2,128,128]{4,3,2,1,0:T(8,128)S(1)}, u32[]{:S(2)}, u32[]{:S(2)}) collective-permute-start(f32[1,2,2,128,128]{4,3,2,1,0:T(8,128)S(1)} %get-tuple-element.57), channel_id=1, source_target_pairs={{0,6},{2,4},{4,2},{6,0},{8,14},{10,12},{12,10},{14,8},{16,22},{18,... | collective-permute-start | bytes 786440 | tf_op jit(solution)/shard_map/ppermute | solution.py:374
  27.4 0.0 copy-done
  27.4 4.8 %shard_map.92 = (bf16[256,2048]{1,0:T(8,128)(2,1)}, bf16[256,2048]{1,0:T(8,128)(2,1)}) custom-call(s32[2]{0:T(128)} %plan_ref.11, bf16[2,256,2048]{2,1,0:T(8,128)(2,1)} %q_ref.7, bf16[2,256,2048]{2,1,0:T(8,128)(2,1)} %k_ref.7, f32[2,16,256]{2,1,0:T(8,128)} %gate_ref.7, f32[16]{0:T(128)} %rate_ref.7, bf16[16,256,256]{2,1,0:T(8,128)(2,1)} %get-tuple-element.30.t_ref), custom_call_target="tpu_custom_call" | custom-call | flops 2147483648 | bytes 8388608 | tf_op jit(solution)/shard_map/pallas_call | solution.py:269
  32.2 18.6 %collective-permute-done.6.refs_7_.refs_8_ = f32[1,2,2,128,128]{4,3,2,1,0:T(8,128)S(1)} collective-permute-done((f32[1,2,2,128,128]{4,3,2,1,0:T(8,128)}, f32[1,2,2,128,128]{4,3,2,1,0:T(8,128)S(1)}, u32[]{:S(2)}, u32[]{:S(2)}) %collective-permute-start.6) | collective-permute-done | bytes 262176 | tf_op jit(solution)/shard_map/ppermute | solution.py:374
  50.9 0.6 collective-permute-start.1
  51.4 3.5 %collective-permute-done.5.refs_6_.refs_7_ = f32[1,2,2,128,128]{4,3,2,1,0:T(8,128)S(1)} collective-permute-done((f32[1,2,2,128,128]{4,3,2,1,0:T(8,128)}, f32[1,2,2,128,128]{4,3,2,1,0:T(8,128)S(1)}, u32[]{:S(2)}, u32[]{:S(2)}) %collective-permute-start.5) | collective-permute-done | bytes 262176 | tf_op jit(solution)/shard_map/ppermute | solution.py:374
  54.9 3.3 %collective-permute-start = (f32[1,2,2,128,128]{4,3,2,1,0:T(8,128)S(1)}, f32[1,2,2,128,128]{4,3,2,1,0:T(8,128)S(1)}, u32[]{:S(2)}, u32[]{:S(2)}) collective-permute-start(f32[1,2,2,128,128]{4,3,2,1,0:T(8,128)S(1)} %get-tuple-element.59), channel_id=1, source_target_pairs={{0,2},{2,0},{4,6},{6,4},{8,10},{10,8},{12,14},{14,12},{16,18},{18,... | collective-permute-start | bytes 786440 | tf_op jit(solution)/shard_map/ppermute | solution.py:374
  58.2 0.1 pad_add_fusion.1.info_ref
  58.3 4.9 %shard_map.94 = (bf16[256,2048]{1,0:T(8,128)(2,1)}, bf16[256,2048]{1,0:T(8,128)(2,1)}) custom-call(s32[2]{0:T(128)} %plan_ref.11, bf16[2,256,2048]{2,1,0:T(8,128)(2,1)} %q_ref.7, bf16[2,256,2048]{2,1,0:T(8,128)(2,1)} %k_ref.7, f32[2,16,256]{2,1,0:T(8,128)} %gate_ref.7, f32[16]{0:T(128)} %rate_ref.7, bf16[16,256,256]{2,1,0:T(8,128)(2,1)} %get-tuple-element.33.t_ref), custom_call_target="tpu_custom_call" | custom-call | flops 2147483648 | bytes 8388608 | tf_op jit(solution)/shard_map/pallas_call | solution.py:269
  63.1 0.0 collective-permute-done.4.refs_5_.refs_6_
  63.1 0.0 collective-permute-done.3.refs_4_.refs_5_
  63.1 0.0 collective-permute-done.2.refs_3_.refs_4_
  63.2 0.0 collective-permute-done.1.refs_2_.refs_3_
  63.2 3.5 %collective-permute-done.refs_1_.refs_2_ = f32[1,2,2,128,128]{4,3,2,1,0:T(8,128)S(1)} collective-permute-done((f32[1,2,2,128,128]{4,3,2,1,0:T(8,128)S(1)}, f32[1,2,2,128,128]{4,3,2,1,0:T(8,128)S(1)}, u32[]{:S(2)}, u32[]{:S(2)}) %collective-permute-start) | collective-permute-done | bytes 262176 | tf_op jit(solution)/shard_map/ppermute | solution.py:374
  66.6 1.8 %shard_map.95 = f32[2,128,128]{2,1,0:T(8,128)S(1)} custom-call(s32[3]{0:T(128)S(1)} %pad_add_fusion.1.info_ref, f32[2,128,128]{2,1,0:T(8,128)S(1)} %constant_dynamic-slice_fusion.start_ref, f32[1,2,2,128,128]{4,3,2,1,0:T(8,128)S(1)} %get-tuple-element.38.refs_0_.refs_1_, f32[1,2,2,128,128]{4,3,2,1,0:T(8,128)S(1)} %collective-permute-done.refs_1_.refs_2_, ...), custom_call_target="tpu_custom_call" | custom-call | flops 201326592 | bytes 3145728 | tf_op jit(solution)/shard_map/pallas_call | solution.py:311
  68.5 4.5 %collective-permute-start.7 = (f32[2,128,128]{2,1,0:T(8,128)S(1)}, f32[2,128,128]{2,1,0:T(8,128)S(1)}, u32[]{:S(2)}, u32[]{:S(2)}) collective-permute-start(f32[2,128,128]{2,1,0:T(8,128)S(1)} %shard_map.95), channel_id=1, source_target_pairs={{0,16},{2,18},{4,20},{6,22},{8,24},{10,26},{12,28},{14,30},{1,17},... | collective-permute-start | bytes 393224 | tf_op jit(solution)/shard_map/ppermute | solution.py:386
  73.0 3.0 %collective-permute-done.7.refs_0_ = f32[2,128,128]{2,1,0:T(8,128)S(1)} collective-permute-done((f32[2,128,128]{2,1,0:T(8,128)S(1)}, f32[2,128,128]{2,1,0:T(8,128)S(1)}, u32[]{:S(2)}, u32[]{:S(2)}) %collective-permute-start.7) | collective-permute-done | bytes 131104 | tf_op jit(solution)/shard_map/ppermute | solution.py:386
  75.9 2.4 %shard_map.96 = f32[8,2,128,128]{3,2,1,0:T(8,128)} custom-call(s32[3]{0:T(128)S(1)} %pad_add_fusion.1.info_ref, f32[2,128,128]{2,1,0:T(8,128)S(1)} %constant_dynamic-slice_fusion.start_ref, f32[2,128,128]{2,1,0:T(8,128)S(1)} %collective-permute-done.7.refs_0_, f32[1,2,2,128,128]{4,3,2,1,0:T(8,128)S(1)} %get-tuple-element.38.refs_0_.refs_1_, ...), custom_call_target="tpu_custom_call" | custom-call | flops 201326592 | bytes 3145728 | tf_op jit(solution)/shard_map/pallas_call | solution.py:311
  78.4 0.0 all-to-all-done.1.refs_0_.refs_1_
  78.4 4.8 %all-to-all-start = ((f32[8,2,128,128]{3,2,1,0:T(8,128)}), f32[8,2,128,128]{3,2,1,0:T(8,128)S(1)}, u32[]{:S(2)}, u32[]{:S(2)}) async-start(f32[8,2,128,128]{3,2,1,0:T(8,128)} %shard_map.96), calls=%async_computation | async-start | bytes 2097152 | tf_op jit(solution)/shard_map/all_to_all | solution.py:371
  83.1 0.1 pad_add_fusion.info_ref
  83.2 2.8 %shard_map.98 = f32[2,128,128]{2,1,0:T(8,128)S(1)} custom-call(s32[3]{0:T(128)S(1)} %pad_add_fusion.info_ref, f32[2,128,128]{2,1,0:T(8,128)S(1)} %constant_dynamic-slice_fusion.start_ref, f32[8,2,2,128,128]{4,3,2,1,0:T(8,128)} %all-to-all-done.1.refs_0_.refs_1_), custom_call_target="tpu_custom_call" | custom-call | flops 201326592 | bytes 3145728 | tf_op jit(solution)/shard_map/pallas_call | solution.py:311
  86.0 5.3 %collective-permute-start.9 = (f32[2,128,128]{2,1,0:T(8,128)S(1)}, f32[2,128,128]{2,1,0:T(8,128)S(1)}, u32[]{:S(2)}, u32[]{:S(2)}) collective-permute-start(f32[2,128,128]{2,1,0:T(8,128)S(1)} %shard_map.98), channel_id=1, source_target_pairs={{0,16},{2,18},{4,20},{6,22},{8,24},{10,26},{12,28},{14,30},{1,17},... | collective-permute-start | bytes 393224 | tf_op jit(solution)/shard_map/ppermute | solution.py:386
  91.3 5.7 %collective-permute-done.9.refs_0_ = f32[2,128,128]{2,1,0:T(8,128)S(1)} collective-permute-done((f32[2,128,128]{2,1,0:T(8,128)S(1)}, f32[2,128,128]{2,1,0:T(8,128)S(1)}, u32[]{:S(2)}, u32[]{:S(2)}) %collective-permute-start.9) | collective-permute-done | bytes 131104 | tf_op jit(solution)/shard_map/ppermute | solution.py:386
  97.0 3.4 %shard_map.99 = f32[8,2,128,128]{3,2,1,0:T(8,128)} custom-call(s32[3]{0:T(128)S(1)} %pad_add_fusion.info_ref, f32[2,128,128]{2,1,0:T(8,128)S(1)} %constant_dynamic-slice_fusion.start_ref, f32[2,128,128]{2,1,0:T(8,128)S(1)} %collective-permute-done.9.refs_0_, f32[8,2,2,128,128]{4,3,2,1,0:T(8,128)} %all-to-all-done.1.refs_0_.refs_1_), custom_call_target="tpu_custom_call" | custom-call | flops 201326592 | bytes 3145728 | tf_op jit(solution)/shard_map/pallas_call | solution.py:311
  100.4 0.0 all-to-all-done.refs_0_.refs_1_.refs_2_.refs_3_.refs_4_.refs_5_.refs_6_.refs_7_
  100.4 3.9 %all-to-all-start.2 = ((f32[8,2,128,128]{3,2,1,0:T(8,128)}), f32[8,2,128,128]{3,2,1,0:T(8,128)S(1)}, u32[]{:S(2)}, u32[]{:S(2)}) async-start(f32[8,2,128,128]{3,2,1,0:T(8,128)} %shard_map.99), calls=%async_computation.2 | async-start | bytes 2097152 | tf_op jit(solution)/shard_map/all_to_all | solution.py:371
  104.3 11.0 %shard_map.97 = (f32[128,4096]{1,0:T(8,128)}, f32[128,4096]{1,0:T(8,128)}) custom-call(s32[2]{0:T(128)} %plan_ref.11, s32[1]{0:T(128)} %bitcast.me_ref, s32[1]{0:T(128)} %constant.16.clone.1.rot_ref, bf16[2,256,2048]{2,1,0:T(8,128)(2,1)} %q_ref.7, bf16[256,2048]{1,0:T(8,128)(2,1)} %get-tuple-element.36.less_ref, ...), custom_call_target="tpu_custom_call" | custom-call | flops 4294967296 | bytes 20971520 | tf_op jit(solution)/shard_map/pallas_call | solution.py:331
  115.4 0.1 collective-permute-start.8
  115.4 2.2 %all-to-all-done.2.refs_0_.refs_1_.refs_2_.refs_3_.refs_4_.refs_5_.refs_6_.refs_7_ = f32[8,2,128,128]{3,2,1,0:T(8,128)S(1)} async-done(((f32[8,2,128,128]{3,2,1,0:T(8,128)}), f32[8,2,128,128]{3,2,1,0:T(8,128)S(1)}, u32[]{:S(2)}, u32[]{:S(2)}) %all-to-all-start.2) | async-done | bytes 1048608 | tf_op jit(solution)/shard_map/all_to_all | solution.py:371
  117.6 0.0 copy-start.1
  117.6 10.1 %shard_map.100 = (f32[128,4096]{1,0:T(8,128)S(1)}, f32[128,4096]{1,0:T(8,128)S(1)}) custom-call(s32[2]{0:T(128)} %plan_ref.11, s32[1]{0:T(128)} %bitcast.me_ref, s32[1]{0:T(128)} %constant.16.clone.1.rot_ref, bf16[2,256,2048]{2,1,0:T(8,128)(2,1)} %q_ref.7, bf16[256,2048]{1,0:T(8,128)(2,1)} %get-tuple-element.48.less_ref, ...), custom_call_target="tpu_custom_call" | custom-call | flops 4294967296 | bytes 20971520 | tf_op jit(solution)/shard_map/pallas_call | solution.py:331
  127.7 0.1 collective-permute-start.10
  127.8 0.0 collective-permute-done.8.refs_1_
  127.8 4.1 %collective-permute-done.10.refs_3_ = f32[128,4096]{1,0:T(8,128)S(1)} collective-permute-done((f32[128,4096]{1,0:T(8,128)S(1)}, f32[128,4096]{1,0:T(8,128)S(1)}, u32[]{:S(2)}, u32[]{:S(2)}) %collective-permute-start.10) | collective-permute-done | bytes 2097184 | tf_op jit(solution)/shard_map/ppermute | solution.py:392
  131.9 0.0 copy-done.1
  131.9 3.2 %sums.1 = bf16[128,2,4096]{2,1,0:T(2,128)(2,1)} custom-call(f32[128,4096]{1,0:T(8,128)S(1)} %copy-done.1, f32[128,4096]{1,0:T(8,128)} %collective-permute-done.8.refs_1_, f32[128,4096]{1,0:T(8,128)S(1)} %get-tuple-element.51.refs_2_, f32[128,4096]{1,0:T(8,128)S(1)} %collective-permute-done.10.refs_3_), custom_call_target="tpu_custom_call" | custom-call | flops 536870912 | bytes 8388608 | tf_op jit(solution)/shard_map/sums/pallas_call | solution.py:395
  (1 shorter events, 0.0 us)
Async XLA Ops:
  0.0 27.4 %copy-start = (f32[16,128,128]{2,1,0:T(8,128)S(1)}, f32[16,128,128]{2,1,0:T(8,128)}, u32[]{:S(2)}) copy-start(f32[16,128,128]{2,1,0:T(8,128)} %param.14) | copy-start | bytes 3145732
  5.9 72.4 %all-to-all-start.1 = ((f32[8,2,2,128,128]{4,3,2,1,0:T(8,128)}), f32[8,2,2,128,128]{4,3,2,1,0:T(8,128)}, u32[]{:S(2)}, u32[]{:S(2)}) async-start(f32[8,2,2,128,128]{4,3,2,1,0:T(8,128)} %get-tuple-element.50), calls=%async_computation.1 | async-start | bytes 4194304 | tf_op jit(solution)/shard_map/all_to_all | solution.py:371
  18.6 32.2 %collective-permute-start.6 = (f32[1,2,2,128,128]{4,3,2,1,0:T(8,128)}, f32[1,2,2,128,128]{4,3,2,1,0:T(8,128)S(1)}, u32[]{:S(2)}, u32[]{:S(2)}) collective-permute-start(f32[1,2,2,128,128]{4,3,2,1,0:T(8,128)} %get-tuple-element.53), channel_id=1, source_target_pairs={{0,14},{2,12},{4,10},{6,8},{8,6},{10,4},{12,2},{14,0},{16,30},{18,... | collective-permute-start | bytes 786440 | tf_op jit(solution)/shard_map/ppermute | solution.py:374
  22.4 32.5 %collective-permute-start.5 = (f32[1,2,2,128,128]{4,3,2,1,0:T(8,128)}, f32[1,2,2,128,128]{4,3,2,1,0:T(8,128)S(1)}, u32[]{:S(2)}, u32[]{:S(2)}) collective-permute-start(f32[1,2,2,128,128]{4,3,2,1,0:T(8,128)} %get-tuple-element.54), channel_id=1, source_target_pairs={{0,12},{2,14},{4,8},{6,10},{8,4},{10,6},{12,0},{14,2},{16,28},{18,... | collective-permute-start | bytes 786440 | tf_op jit(solution)/shard_map/ppermute | solution.py:374
  23.0 40.2 %collective-permute-start.4 = (f32[1,2,2,128,128]{4,3,2,1,0:T(8,128)}, f32[1,2,2,128,128]{4,3,2,1,0:T(8,128)S(1)}, u32[]{:S(2)}, u32[]{:S(2)}) collective-permute-start(f32[1,2,2,128,128]{4,3,2,1,0:T(8,128)} %get-tuple-element.55), channel_id=1, source_target_pairs={{0,10},{2,8},{4,14},{6,12},{8,2},{10,0},{12,6},{14,4},{16,26},{18,... | collective-permute-start | bytes 786440 | tf_op jit(solution)/shard_map/ppermute | solution.py:374
  24.5 38.7 %collective-permute-start.3 = (f32[1,2,2,128,128]{4,3,2,1,0:T(8,128)}, f32[1,2,2,128,128]{4,3,2,1,0:T(8,128)S(1)}, u32[]{:S(2)}, u32[]{:S(2)}) collective-permute-start(f32[1,2,2,128,128]{4,3,2,1,0:T(8,128)} %get-tuple-element.56), channel_id=1, source_target_pairs={{0,8},{2,10},{4,12},{6,14},{8,0},{10,2},{12,4},{14,6},{16,24},{18,... | collective-permute-start | bytes 786440 | tf_op jit(solution)/shard_map/ppermute | solution.py:374
  24.5 38.7 %collective-permute-start.2 = (f32[1,2,2,128,128]{4,3,2,1,0:T(8,128)S(1)}, f32[1,2,2,128,128]{4,3,2,1,0:T(8,128)S(1)}, u32[]{:S(2)}, u32[]{:S(2)}) collective-permute-start(f32[1,2,2,128,128]{4,3,2,1,0:T(8,128)S(1)} %get-tuple-element.57), channel_id=1, source_target_pairs={{0,6},{2,4},{4,2},{6,0},{8,14},{10,12},{12,10},{14,8},{16,22},{18,... | collective-permute-start | bytes 786440 | tf_op jit(solution)/shard_map/ppermute | solution.py:374
  50.9 12.3 %collective-permute-start.1 = (f32[1,2,2,128,128]{4,3,2,1,0:T(8,128)S(1)}, f32[1,2,2,128,128]{4,3,2,1,0:T(8,128)S(1)}, u32[]{:S(2)}, u32[]{:S(2)}) collective-permute-start(f32[1,2,2,128,128]{4,3,2,1,0:T(8,128)S(1)} %get-tuple-element.58), channel_id=1, source_target_pairs={{0,4},{2,6},{4,0},{6,2},{8,12},{10,14},{12,8},{14,10},{16,20},{18,... | collective-permute-start | bytes 786440 | tf_op jit(solution)/shard_map/ppermute | solution.py:374
  54.9 11.7 %collective-permute-start = (f32[1,2,2,128,128]{4,3,2,1,0:T(8,128)S(1)}, f32[1,2,2,128,128]{4,3,2,1,0:T(8,128)S(1)}, u32[]{:S(2)}, u32[]{:S(2)}) collective-permute-start(f32[1,2,2,128,128]{4,3,2,1,0:T(8,128)S(1)} %get-tuple-element.59), channel_id=1, source_target_pairs={{0,2},{2,0},{4,6},{6,4},{8,10},{10,8},{12,14},{14,12},{16,18},{18,... | collective-permute-start | bytes 786440 | tf_op jit(solution)/shard_map/ppermute | solution.py:374
  68.5 7.5 %collective-permute-start.7 = (f32[2,128,128]{2,1,0:T(8,128)S(1)}, f32[2,128,128]{2,1,0:T(8,128)S(1)}, u32[]{:S(2)}, u32[]{:S(2)}) collective-permute-start(f32[2,128,128]{2,1,0:T(8,128)S(1)} %shard_map.95), channel_id=1, source_target_pairs={{0,16},{2,18},{4,20},{6,22},{8,24},{10,26},{12,28},{14,30},{1,17},... | collective-permute-start | bytes 393224 | tf_op jit(solution)/shard_map/ppermute | solution.py:386
  78.4 22.0 %all-to-all-start = ((f32[8,2,128,128]{3,2,1,0:T(8,128)}), f32[8,2,128,128]{3,2,1,0:T(8,128)S(1)}, u32[]{:S(2)}, u32[]{:S(2)}) async-start(f32[8,2,128,128]{3,2,1,0:T(8,128)} %shard_map.96), calls=%async_computation | async-start | bytes 2097152 | tf_op jit(solution)/shard_map/all_to_all | solution.py:371
  86.0 11.0 %collective-permute-start.9 = (f32[2,128,128]{2,1,0:T(8,128)S(1)}, f32[2,128,128]{2,1,0:T(8,128)S(1)}, u32[]{:S(2)}, u32[]{:S(2)}) collective-permute-start(f32[2,128,128]{2,1,0:T(8,128)S(1)} %shard_map.98), channel_id=1, source_target_pairs={{0,16},{2,18},{4,20},{6,22},{8,24},{10,26},{12,28},{14,30},{1,17},... | collective-permute-start | bytes 393224 | tf_op jit(solution)/shard_map/ppermute | solution.py:386
  100.4 17.2 %all-to-all-start.2 = ((f32[8,2,128,128]{3,2,1,0:T(8,128)}), f32[8,2,128,128]{3,2,1,0:T(8,128)S(1)}, u32[]{:S(2)}, u32[]{:S(2)}) async-start(f32[8,2,128,128]{3,2,1,0:T(8,128)} %shard_map.99), calls=%async_computation.2 | async-start | bytes 2097152 | tf_op jit(solution)/shard_map/all_to_all | solution.py:371
  115.4 12.4 %collective-permute-start.8 = (f32[128,4096]{1,0:T(8,128)}, f32[128,4096]{1,0:T(8,128)}, u32[]{:S(2)}, u32[]{:S(2)}) collective-permute-start(f32[128,4096]{1,0:T(8,128)} %get-tuple-element.47), channel_id=1, source_target_pairs={{0,1},{1,0},{2,3},{3,2},{4,5},{5,4},{6,7},{7,6},{8,9},{9,8},{10,11... | collective-permute-start | bytes 6291464 | tf_op jit(solution)/shard_map/ppermute | solution.py:392
  117.6 14.3 %copy-start.1 = (f32[128,4096]{1,0:T(8,128)S(1)}, f32[128,4096]{1,0:T(8,128)}, u32[]{:S(2)}) copy-start(f32[128,4096]{1,0:T(8,128)} %get-tuple-element.46.refs_0_) | copy-start | bytes 6291460
  127.7 4.2 %collective-permute-start.10 = (f32[128,4096]{1,0:T(8,128)S(1)}, f32[128,4096]{1,0:T(8,128)S(1)}, u32[]{:S(2)}, u32[]{:S(2)}) collective-permute-start(f32[128,4096]{1,0:T(8,128)S(1)} %get-tuple-element.52), channel_id=1, source_target_pairs={{0,1},{1,0},{2,3},{3,2},{4,5},{5,4},{6,7},{7,6},{8,9},{9,8},{10,11... | collective-permute-start | bytes 6291464 | tf_op jit(solution)/shard_map/ppermute | solution.py:392

commit v3 on v2

--- a/solution.py
+++ b/solution.py
@@ -290,10 +290,11 @@
 
     start = lax.dynamic_slice_in_dim(init_state, place * per, per)
 
-    def chain(s, gathered, moved, all_out):
+    def chain(s, gathered, moved, all_out, far):
         shape = (group, per, HS, HS) if all_out else (per, HS, HS)
         info = jnp.concatenate([rots[UP_PERMUTE[s]], block.reshape(1), rots[DOWN_PERMUTE[s]]])
-        kind = "pieces" if isinstance(gathered, list) else "far" if s else "near"
+        kind = "pieces" if isinstance(gathered, list) else "far" if far else "near"
+        keeps = kind == "far" and not all_out
         hops = moved is not None
         given = [start, moved] if hops else [start]
         vmem, hbm = pl.BlockSpec(memory_space=pltpu.VMEM), pl.BlockSpec(memory_space=pltpu.HBM)
@@ -303,7 +304,7 @@
         given += [in_hbm(x) if kind == "far" else in_vmem(x) for x in pieces]
         specs += [hbm if kind == "far" else vmem] * len(pieces)
         streamed = all_out and not DOWN_PERMUTE[s]
-        scratch = [] if kind == "near" else [pltpu.VMEM((group, per, 2, HS, HS), F32)]
+        scratch = [] if kind == "near" or keeps else [pltpu.VMEM((group, per, 2, HS, HS), F32)]
         if kind == "far":
             scratch.append(pltpu.SemaphoreType.DMA((group,)))
         if streamed:
@@ -311,9 +312,10 @@
         return pl.pallas_call(
             functools.partial(chain_kernel, group, hops, all_out, kind, streamed),
             in_specs=specs,
-            out_specs=hbm if streamed else vmem,
+            out_specs=[hbm if streamed else vmem] + [vmem] * keeps,
             scratch_shapes=scratch,
-            out_shape=pltpu.HBM(shape, F32) if streamed else jax.ShapeDtypeStruct(shape, F32),
+            out_shape=[pltpu.HBM(shape, F32) if streamed else jax.ShapeDtypeStruct(shape, F32)]
+            + [pltpu.VMEM((group, per, 2, HS, HS), F32)] * keeps,
             compiler_params=limit(SMALL),
             cost_estimate=cost(group * per * 6 * HS**3, group * per * HS * HS * 12),
         )(info, *given)
@@ -380,11 +382,12 @@
     gathered[0], reads = lax.optimization_barrier((gathered[0], reads))
     outs = []
     for s in range(seqs):
-        moved = None
+        moved, held, far = None, gathered[s], s > 0
         for _ in range(ctx // group - 1):
-            ending = chain(s, gathered[s], moved, False)
+            ending, *kept = chain(s, held, moved, False, far)
+            held, far = (kept[0], False) if kept else (held, far)
             moved = lax.ppermute(ending, "ctx", onward)
-        leaving = chain(s, gathered[s], moved, True)
+        (leaving,) = chain(s, held, moved, True, far)
         entering = shared(leaving, DOWN_PERMUTE[s])
         products = final_of(s, reads[s], entering)
         outs.append(products[0])

time: 136 us -> 135 us (level)
  no operation moved by 1% of the time
where the time goes in v3:
time: 135 us; the launch traced here: 134 us
  Pallas kernels  54.6 us (40%)
  waiting for transfers between devices  40.6 us (30%)
  starting transfers between devices  37.5 us (28%)
    ppermute x7, waiting for transfers between devices, shared(): lax.ppermute(pieces[d:d + 1], 'ctx', [(i, i ^ d) for i in range(ctx)])  25.6 us
    pallas_call x2, Pallas kernels, final_of(): pl.pallas_call(functools.partial(final_kernel, steps, parts, group), grid...  21.1 us
    all_to_all x3, starting transfers between devices, shared(): lax.all_to_all(pieces, 'ctx', 0, 0, tiled=True, axis_index_groups=groups)  14.9 us
    ppermute x7, starting transfers between devices, shared(): lax.ppermute(pieces[d:d + 1], 'ctx', [(i, i ^ d) for i in range(ctx)])  12.6 us
    pallas_call x2, Pallas kernels, maps_of(): pl.pallas_call(functools.partial(maps_kernel, step, per), grid_spec=grid_...  11.3 us
    ppermute x2, starting transfers between devices, per_device(): moved = lax.ppermute(ending, 'ctx', onward)  9.77 us
    pallas_call x2, Pallas kernels, reads_of(): pl.pallas_call(functools.partial(reads_kernel, step), grid_spec=pltpu.Pre...  9.63 us
    pallas_call x4, Pallas kernels, chain(): pl.pallas_call(functools.partial(chain_kernel, group, hops, all_out, kind...  9.32 us
  transfers between devices with their start and end apart: 14, of which 7 were waited for; matrix products, arithmetic and copies ran while one was open for 1% of the time, Pallas kernels for 34%

profile of v3, /device:TPU:0, one launch (start us, length us, event | category | flops | bytes accessed | tf_op | source)
XLA Modules:
  0.0 134.0 jit_solution(16260800732349789057)
XLA Ops:
  0.0 0.0 copy-start
  0.0 5.9 %shard_map.93 = (f32[8,2,2,128,128]{4,3,2,1,0:T(8,128)}, bf16[16,256,256]{2,1,0:T(8,128)(2,1)}) custom-call(s32[2]{0:T(128)} %plan_ref.11, s32[1]{0:T(128)} %constant.16.clone.1.rot_ref, bf16[2,256,2048]{2,1,0:T(8,128)(2,1)} %k_ref.7, bf16[2,256,2048]{2,1,0:T(8,128)(2,1)} %v_ref.3, f32[2,16,256]{2,1,0:T(8,128)} %gate_ref.7, f32[16]{0:T(128)} %rate_ref.7), custom_call_target="tpu_custom_call" | custom-call | flops 1610612736 | bytes 6291456 | tf_op jit(solution)/shard_map/pallas_call | solution.py:257
  5.9 6.2 %all-to-all-start.1 = ((f32[8,2,2,128,128]{4,3,2,1,0:T(8,128)}), f32[8,2,2,128,128]{4,3,2,1,0:T(8,128)}, u32[]{:S(2)}, u32[]{:S(2)}) async-start(f32[8,2,2,128,128]{4,3,2,1,0:T(8,128)} %get-tuple-element.52), calls=%async_computation.1 | async-start | bytes 4194304 | tf_op jit(solution)/shard_map/all_to_all | solution.py:373
  12.2 5.4 %shard_map.91 = (f32[8,2,2,128,128]{4,3,2,1,0:T(8,128)S(1)}, bf16[16,256,256]{2,1,0:T(8,128)(2,1)}) custom-call(s32[2]{0:T(128)} %plan_ref.11, s32[1]{0:T(128)} %bitcast.1.rot_ref, bf16[2,256,2048]{2,1,0:T(8,128)(2,1)} %k_ref.7, bf16[2,256,2048]{2,1,0:T(8,128)(2,1)} %v_ref.3, f32[2,16,256]{2,1,0:T(8,128)} %gate_ref.7, f32[16]{0:T(128)} %rate_ref.7), custom_call_target="tpu_custom_call" | custom-call | flops 1610612736 | bytes 6291456 | tf_op jit(solution)/shard_map/pallas_call | solution.py:257
  17.5 1.1 fusion
  18.6 3.8 %collective-permute-start.6 = (f32[1,2,2,128,128]{4,3,2,1,0:T(8,128)}, f32[1,2,2,128,128]{4,3,2,1,0:T(8,128)S(1)}, u32[]{:S(2)}, u32[]{:S(2)}) collective-permute-start(f32[1,2,2,128,128]{4,3,2,1,0:T(8,128)} %get-tuple-element.57), channel_id=1, source_target_pairs={{0,14},{2,12},{4,10},{6,8},{8,6},{10,4},{12,2},{14,0},{16,30},{18,... | collective-permute-start | bytes 786440 | tf_op jit(solution)/shard_map/ppermute | solution.py:376
  22.4 0.6 collective-permute-start.5
  23.0 1.5 %collective-permute-start.4 = (f32[1,2,2,128,128]{4,3,2,1,0:T(8,128)}, f32[1,2,2,128,128]{4,3,2,1,0:T(8,128)S(1)}, u32[]{:S(2)}, u32[]{:S(2)}) collective-permute-start(f32[1,2,2,128,128]{4,3,2,1,0:T(8,128)} %get-tuple-element.59), channel_id=1, source_target_pairs={{0,10},{2,8},{4,14},{6,12},{8,2},{10,0},{12,6},{14,4},{16,26},{18,... | collective-permute-start | bytes 786440 | tf_op jit(solution)/shard_map/ppermute | solution.py:376
  24.5 0.0 collective-permute-start.3
  24.5 2.9 %collective-permute-start.2 = (f32[1,2,2,128,128]{4,3,2,1,0:T(8,128)S(1)}, f32[1,2,2,128,128]{4,3,2,1,0:T(8,128)S(1)}, u32[]{:S(2)}, u32[]{:S(2)}) collective-permute-start(f32[1,2,2,128,128]{4,3,2,1,0:T(8,128)S(1)} %get-tuple-element.61), channel_id=1, source_target_pairs={{0,6},{2,4},{4,2},{6,0},{8,14},{10,12},{12,10},{14,8},{16,22},{18,... | collective-permute-start | bytes 786440 | tf_op jit(solution)/shard_map/ppermute | solution.py:376
  27.4 0.0 copy-done
  27.4 4.9 %shard_map.92 = (bf16[256,2048]{1,0:T(8,128)(2,1)}, bf16[256,2048]{1,0:T(8,128)(2,1)}) custom-call(s32[2]{0:T(128)} %plan_ref.11, bf16[2,256,2048]{2,1,0:T(8,128)(2,1)} %q_ref.7, bf16[2,256,2048]{2,1,0:T(8,128)(2,1)} %k_ref.7, f32[2,16,256]{2,1,0:T(8,128)} %gate_ref.7, f32[16]{0:T(128)} %rate_ref.7, bf16[16,256,256]{2,1,0:T(8,128)(2,1)} %get-tuple-element.32.t_ref), custom_call_target="tpu_custom_call" | custom-call | flops 2147483648 | bytes 8388608 | tf_op jit(solution)/shard_map/pallas_call | solution.py:269
  32.3 18.6 %collective-permute-done.6.refs_7_.refs_8_ = f32[1,2,2,128,128]{4,3,2,1,0:T(8,128)S(1)} collective-permute-done((f32[1,2,2,128,128]{4,3,2,1,0:T(8,128)}, f32[1,2,2,128,128]{4,3,2,1,0:T(8,128)S(1)}, u32[]{:S(2)}, u32[]{:S(2)}) %collective-permute-start.6) | collective-permute-done | bytes 262176 | tf_op jit(solution)/shard_map/ppermute | solution.py:376
  50.9 0.6 collective-permute-start.1
  51.4 3.5 %collective-permute-done.5.refs_6_.refs_7_ = f32[1,2,2,128,128]{4,3,2,1,0:T(8,128)S(1)} collective-permute-done((f32[1,2,2,128,128]{4,3,2,1,0:T(8,128)}, f32[1,2,2,128,128]{4,3,2,1,0:T(8,128)S(1)}, u32[]{:S(2)}, u32[]{:S(2)}) %collective-permute-start.5) | collective-permute-done | bytes 262176 | tf_op jit(solution)/shard_map/ppermute | solution.py:376
  54.9 3.3 %collective-permute-start = (f32[1,2,2,128,128]{4,3,2,1,0:T(8,128)S(1)}, f32[1,2,2,128,128]{4,3,2,1,0:T(8,128)S(1)}, u32[]{:S(2)}, u32[]{:S(2)}) collective-permute-start(f32[1,2,2,128,128]{4,3,2,1,0:T(8,128)S(1)} %get-tuple-element.63), channel_id=1, source_target_pairs={{0,2},{2,0},{4,6},{6,4},{8,10},{10,8},{12,14},{14,12},{16,18},{18,... | collective-permute-start | bytes 786440 | tf_op jit(solution)/shard_map/ppermute | solution.py:376
  58.2 0.1 pad_add_fusion.1.info_ref
  58.3 4.8 %shard_map.94 = (bf16[256,2048]{1,0:T(8,128)(2,1)}, bf16[256,2048]{1,0:T(8,128)(2,1)}) custom-call(s32[2]{0:T(128)} %plan_ref.11, bf16[2,256,2048]{2,1,0:T(8,128)(2,1)} %q_ref.7, bf16[2,256,2048]{2,1,0:T(8,128)(2,1)} %k_ref.7, f32[2,16,256]{2,1,0:T(8,128)} %gate_ref.7, f32[16]{0:T(128)} %rate_ref.7, bf16[16,256,256]{2,1,0:T(8,128)(2,1)} %get-tuple-element.35.t_ref), custom_call_target="tpu_custom_call" | custom-call | flops 2147483648 | bytes 8388608 | tf_op jit(solution)/shard_map/pallas_call | solution.py:269
  63.0 0.0 collective-permute-done.4.refs_5_.refs_6_
  63.0 0.0 collective-permute-done.3.refs_4_.refs_5_
  63.0 0.0 collective-permute-done.2.refs_3_.refs_4_
  63.0 0.0 collective-permute-done.1.refs_2_.refs_3_
  63.1 3.6 %collective-permute-done.refs_1_.refs_2_ = f32[1,2,2,128,128]{4,3,2,1,0:T(8,128)S(1)} collective-permute-done((f32[1,2,2,128,128]{4,3,2,1,0:T(8,128)S(1)}, f32[1,2,2,128,128]{4,3,2,1,0:T(8,128)S(1)}, u32[]{:S(2)}, u32[]{:S(2)}) %collective-permute-start) | collective-permute-done | bytes 262176 | tf_op jit(solution)/shard_map/ppermute | solution.py:376
  66.6 1.8 %shard_map.95 = f32[2,128,128]{2,1,0:T(8,128)S(1)} custom-call(s32[3]{0:T(128)S(1)} %pad_add_fusion.1.info_ref, f32[2,128,128]{2,1,0:T(8,128)S(1)} %constant_dynamic-slice_fusion.start_ref, f32[1,2,2,128,128]{4,3,2,1,0:T(8,128)S(1)} %get-tuple-element.40.refs_0_.refs_1_, f32[1,2,2,128,128]{4,3,2,1,0:T(8,128)S(1)} %collective-permute-done.refs_1_.refs_2_, ...), custom_call_target="tpu_custom_call" | custom-call | flops 201326592 | bytes 3145728 | tf_op jit(solution)/shard_map/pallas_call | solution.py:312
  68.5 4.5 %collective-permute-start.7 = (f32[2,128,128]{2,1,0:T(8,128)S(1)}, f32[2,128,128]{2,1,0:T(8,128)S(1)}, u32[]{:S(2)}, u32[]{:S(2)}) collective-permute-start(f32[2,128,128]{2,1,0:T(8,128)S(1)} %shard_map.95), channel_id=1, source_target_pairs={{0,16},{2,18},{4,20},{6,22},{8,24},{10,26},{12,28},{14,30},{1,17},... | collective-permute-start | bytes 393224 | tf_op jit(solution)/shard_map/ppermute | solution.py:389
  73.0 3.0 %collective-permute-done.7.refs_0_ = f32[2,128,128]{2,1,0:T(8,128)S(1)} collective-permute-done((f32[2,128,128]{2,1,0:T(8,128)S(1)}, f32[2,128,128]{2,1,0:T(8,128)S(1)}, u32[]{:S(2)}, u32[]{:S(2)}) %collective-permute-start.7) | collective-permute-done | bytes 131104 | tf_op jit(solution)/shard_map/ppermute | solution.py:389
  75.9 2.4 %shard_map.96 = f32[8,2,128,128]{3,2,1,0:T(8,128)} custom-call(s32[3]{0:T(128)S(1)} %pad_add_fusion.1.info_ref, f32[2,128,128]{2,1,0:T(8,128)S(1)} %constant_dynamic-slice_fusion.start_ref, f32[2,128,128]{2,1,0:T(8,128)S(1)} %collective-permute-done.7.refs_0_, f32[1,2,2,128,128]{4,3,2,1,0:T(8,128)S(1)} %get-tuple-element.40.refs_0_.refs_1_, ...), custom_call_target="tpu_custom_call" | custom-call | flops 201326592 | bytes 3145728 | tf_op jit(solution)/shard_map/pallas_call | solution.py:312
  78.3 0.0 all-to-all-done.1.refs_0_
  78.4 4.8 %all-to-all-start = ((f32[8,2,128,128]{3,2,1,0:T(8,128)}), f32[8,2,128,128]{3,2,1,0:T(8,128)S(1)}, u32[]{:S(2)}, u32[]{:S(2)}) async-start(f32[8,2,128,128]{3,2,1,0:T(8,128)} %shard_map.96), calls=%async_computation | async-start | bytes 2097152 | tf_op jit(solution)/shard_map/all_to_all | solution.py:373
  83.1 0.1 pad_add_fusion.info_ref
  83.2 2.8 %shard_map.98 = (f32[2,128,128]{2,1,0:T(8,128)S(1)}, f32[8,2,2,128,128]{4,3,2,1,0:T(8,128)S(1)}) custom-call(s32[3]{0:T(128)S(1)} %pad_add_fusion.info_ref, f32[2,128,128]{2,1,0:T(8,128)S(1)} %constant_dynamic-slice_fusion.start_ref, f32[8,2,2,128,128]{4,3,2,1,0:T(8,128)} %all-to-all-done.1.refs_0_), custom_call_target="tpu_custom_call" | custom-call | flops 201326592 | bytes 3145728 | tf_op jit(solution)/shard_map/pallas_call | solution.py:312
  86.0 5.3 %collective-permute-start.9 = (f32[2,128,128]{2,1,0:T(8,128)S(1)}, f32[2,128,128]{2,1,0:T(8,128)S(1)}, u32[]{:S(2)}, u32[]{:S(2)}) collective-permute-start(f32[2,128,128]{2,1,0:T(8,128)S(1)} %get-tuple-element.53), channel_id=1, source_target_pairs={{0,16},{2,18},{4,20},{6,22},{8,24},{10,26},{12,28},{14,30},{1,17},... | collective-permute-start | bytes 393224 | tf_op jit(solution)/shard_map/ppermute | solution.py:389
  91.3 5.7 %collective-permute-done.9.refs_0_ = f32[2,128,128]{2,1,0:T(8,128)S(1)} collective-permute-done((f32[2,128,128]{2,1,0:T(8,128)S(1)}, f32[2,128,128]{2,1,0:T(8,128)S(1)}, u32[]{:S(2)}, u32[]{:S(2)}) %collective-permute-start.9) | collective-permute-done | bytes 131104 | tf_op jit(solution)/shard_map/ppermute | solution.py:389
  97.0 2.3 %shard_map.99 = f32[8,2,128,128]{3,2,1,0:T(8,128)} custom-call(s32[3]{0:T(128)S(1)} %pad_add_fusion.info_ref, f32[2,128,128]{2,1,0:T(8,128)S(1)} %constant_dynamic-slice_fusion.start_ref, f32[2,128,128]{2,1,0:T(8,128)S(1)} %collective-permute-done.9.refs_0_, f32[8,2,2,128,128]{4,3,2,1,0:T(8,128)S(1)} %get-tuple-element.54.refs_1_), custom_call_target="tpu_custom_call" | custom-call | flops 201326592 | bytes 3145728 | tf_op jit(solution)/shard_map/pallas_call | solution.py:312
  99.3 0.0 all-to-all-done.refs_0_.refs_1_.refs_2_.refs_3_.refs_4_.refs_5_.refs_6_.refs_7_
  99.3 3.9 %all-to-all-start.2 = ((f32[8,2,128,128]{3,2,1,0:T(8,128)}), f32[8,2,128,128]{3,2,1,0:T(8,128)S(1)}, u32[]{:S(2)}, u32[]{:S(2)}) async-start(f32[8,2,128,128]{3,2,1,0:T(8,128)} %shard_map.99), calls=%async_computation.2 | async-start | bytes 2097152 | tf_op jit(solution)/shard_map/all_to_all | solution.py:373
  103.2 11.1 %shard_map.97 = (f32[128,4096]{1,0:T(8,128)}, f32[128,4096]{1,0:T(8,128)}) custom-call(s32[2]{0:T(128)} %plan_ref.11, s32[1]{0:T(128)} %bitcast.me_ref, s32[1]{0:T(128)} %constant.16.clone.1.rot_ref, bf16[2,256,2048]{2,1,0:T(8,128)(2,1)} %q_ref.7, bf16[256,2048]{1,0:T(8,128)(2,1)} %get-tuple-element.38.less_ref, ...), custom_call_target="tpu_custom_call" | custom-call | flops 4294967296 | bytes 20971520 | tf_op jit(solution)/shard_map/pallas_call | solution.py:333
  114.3 0.1 collective-permute-start.8
  114.4 2.1 %all-to-all-done.2.refs_0_.refs_1_.refs_2_.refs_3_.refs_4_.refs_5_.refs_6_.refs_7_ = f32[8,2,128,128]{3,2,1,0:T(8,128)S(1)} async-done(((f32[8,2,128,128]{3,2,1,0:T(8,128)}), f32[8,2,128,128]{3,2,1,0:T(8,128)S(1)}, u32[]{:S(2)}, u32[]{:S(2)}) %all-to-all-start.2) | async-done | bytes 1048608 | tf_op jit(solution)/shard_map/all_to_all | solution.py:373
  116.5 0.0 copy-start.1
  116.5 10.1 %shard_map.100 = (f32[128,4096]{1,0:T(8,128)S(1)}, f32[128,4096]{1,0:T(8,128)S(1)}) custom-call(s32[2]{0:T(128)} %plan_ref.11, s32[1]{0:T(128)} %bitcast.me_ref, s32[1]{0:T(128)} %constant.16.clone.1.rot_ref, bf16[2,256,2048]{2,1,0:T(8,128)(2,1)} %q_ref.7, bf16[256,2048]{1,0:T(8,128)(2,1)} %get-tuple-element.50.less_ref, ...), custom_call_target="tpu_custom_call" | custom-call | flops 4294967296 | bytes 20971520 | tf_op jit(solution)/shard_map/pallas_call | solution.py:333
  126.6 0.1 collective-permute-start.10
  126.6 0.0 collective-permute-done.8.refs_1_
  126.7 4.1 %collective-permute-done.10.refs_3_ = f32[128,4096]{1,0:T(8,128)S(1)} collective-permute-done((f32[128,4096]{1,0:T(8,128)S(1)}, f32[128,4096]{1,0:T(8,128)S(1)}, u32[]{:S(2)}, u32[]{:S(2)}) %collective-permute-start.10) | collective-permute-done | bytes 2097184 | tf_op jit(solution)/shard_map/ppermute | solution.py:395
  130.8 0.0 copy-done.1
  130.8 3.2 %sums.1 = bf16[128,2,4096]{2,1,0:T(2,128)(2,1)} custom-call(f32[128,4096]{1,0:T(8,128)S(1)} %copy-done.1, f32[128,4096]{1,0:T(8,128)} %collective-permute-done.8.refs_1_, f32[128,4096]{1,0:T(8,128)S(1)} %get-tuple-element.55.refs_2_, f32[128,4096]{1,0:T(8,128)S(1)} %collective-permute-done.10.refs_3_), custom_call_target="tpu_custom_call" | custom-call | flops 536870912 | bytes 8388608 | tf_op jit(solution)/shard_map/sums/pallas_call | solution.py:398
  (1 shorter events, 0.0 us)
Async XLA Ops:
  0.0 27.4 %copy-start = (f32[16,128,128]{2,1,0:T(8,128)S(1)}, f32[16,128,128]{2,1,0:T(8,128)}, u32[]{:S(2)}) copy-start(f32[16,128,128]{2,1,0:T(8,128)} %param.14) | copy-start | bytes 3145732
  5.9 72.4 %all-to-all-start.1 = ((f32[8,2,2,128,128]{4,3,2,1,0:T(8,128)}), f32[8,2,2,128,128]{4,3,2,1,0:T(8,128)}, u32[]{:S(2)}, u32[]{:S(2)}) async-start(f32[8,2,2,128,128]{4,3,2,1,0:T(8,128)} %get-tuple-element.52), calls=%async_computation.1 | async-start | bytes 4194304 | tf_op jit(solution)/shard_map/all_to_all | solution.py:373
  18.6 32.3 %collective-permute-start.6 = (f32[1,2,2,128,128]{4,3,2,1,0:T(8,128)}, f32[1,2,2,128,128]{4,3,2,1,0:T(8,128)S(1)}, u32[]{:S(2)}, u32[]{:S(2)}) collective-permute-start(f32[1,2,2,128,128]{4,3,2,1,0:T(8,128)} %get-tuple-element.57), channel_id=1, source_target_pairs={{0,14},{2,12},{4,10},{6,8},{8,6},{10,4},{12,2},{14,0},{16,30},{18,... | collective-permute-start | bytes 786440 | tf_op jit(solution)/shard_map/ppermute | solution.py:376
  22.4 32.5 %collective-permute-start.5 = (f32[1,2,2,128,128]{4,3,2,1,0:T(8,128)}, f32[1,2,2,128,128]{4,3,2,1,0:T(8,128)S(1)}, u32[]{:S(2)}, u32[]{:S(2)}) collective-permute-start(f32[1,2,2,128,128]{4,3,2,1,0:T(8,128)} %get-tuple-element.58), channel_id=1, source_target_pairs={{0,12},{2,14},{4,8},{6,10},{8,4},{10,6},{12,0},{14,2},{16,28},{18,... | collective-permute-start | bytes 786440 | tf_op jit(solution)/shard_map/ppermute | solution.py:376
  23.0 40.1 %collective-permute-start.4 = (f32[1,2,2,128,128]{4,3,2,1,0:T(8,128)}, f32[1,2,2,128,128]{4,3,2,1,0:T(8,128)S(1)}, u32[]{:S(2)}, u32[]{:S(2)}) collective-permute-start(f32[1,2,2,128,128]{4,3,2,1,0:T(8,128)} %get-tuple-element.59), channel_id=1, source_target_pairs={{0,10},{2,8},{4,14},{6,12},{8,2},{10,0},{12,6},{14,4},{16,26},{18,... | collective-permute-start | bytes 786440 | tf_op jit(solution)/shard_map/ppermute | solution.py:376
  24.5 38.6 %collective-permute-start.3 = (f32[1,2,2,128,128]{4,3,2,1,0:T(8,128)}, f32[1,2,2,128,128]{4,3,2,1,0:T(8,128)S(1)}, u32[]{:S(2)}, u32[]{:S(2)}) collective-permute-start(f32[1,2,2,128,128]{4,3,2,1,0:T(8,128)} %get-tuple-element.60), channel_id=1, source_target_pairs={{0,8},{2,10},{4,12},{6,14},{8,0},{10,2},{12,4},{14,6},{16,24},{18,... | collective-permute-start | bytes 786440 | tf_op jit(solution)/shard_map/ppermute | solution.py:376
  24.5 38.6 %collective-permute-start.2 = (f32[1,2,2,128,128]{4,3,2,1,0:T(8,128)S(1)}, f32[1,2,2,128,128]{4,3,2,1,0:T(8,128)S(1)}, u32[]{:S(2)}, u32[]{:S(2)}) collective-permute-start(f32[1,2,2,128,128]{4,3,2,1,0:T(8,128)S(1)} %get-tuple-element.61), channel_id=1, source_target_pairs={{0,6},{2,4},{4,2},{6,0},{8,14},{10,12},{12,10},{14,8},{16,22},{18,... | collective-permute-start | bytes 786440 | tf_op jit(solution)/shard_map/ppermute | solution.py:376
  50.9 12.2 %collective-permute-start.1 = (f32[1,2,2,128,128]{4,3,2,1,0:T(8,128)S(1)}, f32[1,2,2,128,128]{4,3,2,1,0:T(8,128)S(1)}, u32[]{:S(2)}, u32[]{:S(2)}) collective-permute-start(f32[1,2,2,128,128]{4,3,2,1,0:T(8,128)S(1)} %get-tuple-element.62), channel_id=1, source_target_pairs={{0,4},{2,6},{4,0},{6,2},{8,12},{10,14},{12,8},{14,10},{16,20},{18,... | collective-permute-start | bytes 786440 | tf_op jit(solution)/shard_map/ppermute | solution.py:376
  54.9 11.7 %collective-permute-start = (f32[1,2,2,128,128]{4,3,2,1,0:T(8,128)S(1)}, f32[1,2,2,128,128]{4,3,2,1,0:T(8,128)S(1)}, u32[]{:S(2)}, u32[]{:S(2)}) collective-permute-start(f32[1,2,2,128,128]{4,3,2,1,0:T(8,128)S(1)} %get-tuple-element.63), channel_id=1, source_target_pairs={{0,2},{2,0},{4,6},{6,4},{8,10},{10,8},{12,14},{14,12},{16,18},{18,... | collective-permute-start | bytes 786440 | tf_op jit(solution)/shard_map/ppermute | solution.py:376
  68.5 7.5 %collective-permute-start.7 = (f32[2,128,128]{2,1,0:T(8,128)S(1)}, f32[2,128,128]{2,1,0:T(8,128)S(1)}, u32[]{:S(2)}, u32[]{:S(2)}) collective-permute-start(f32[2,128,128]{2,1,0:T(8,128)S(1)} %shard_map.95), channel_id=1, source_target_pairs={{0,16},{2,18},{4,20},{6,22},{8,24},{10,26},{12,28},{14,30},{1,17},... | collective-permute-start | bytes 393224 | tf_op jit(solution)/shard_map/ppermute | solution.py:389
  78.4 20.9 %all-to-all-start = ((f32[8,2,128,128]{3,2,1,0:T(8,128)}), f32[8,2,128,128]{3,2,1,0:T(8,128)S(1)}, u32[]{:S(2)}, u32[]{:S(2)}) async-start(f32[8,2,128,128]{3,2,1,0:T(8,128)} %shard_map.96), calls=%async_computation | async-start | bytes 2097152 | tf_op jit(solution)/shard_map/all_to_all | solution.py:373
  86.0 11.0 %collective-permute-start.9 = (f32[2,128,128]{2,1,0:T(8,128)S(1)}, f32[2,128,128]{2,1,0:T(8,128)S(1)}, u32[]{:S(2)}, u32[]{:S(2)}) collective-permute-start(f32[2,128,128]{2,1,0:T(8,128)S(1)} %get-tuple-element.53), channel_id=1, source_target_pairs={{0,16},{2,18},{4,20},{6,22},{8,24},{10,26},{12,28},{14,30},{1,17},... | collective-permute-start | bytes 393224 | tf_op jit(solution)/shard_map/ppermute | solution.py:389
  99.3 17.2 %all-to-all-start.2 = ((f32[8,2,128,128]{3,2,1,0:T(8,128)}), f32[8,2,128,128]{3,2,1,0:T(8,128)S(1)}, u32[]{:S(2)}, u32[]{:S(2)}) async-start(f32[8,2,128,128]{3,2,1,0:T(8,128)} %shard_map.99), calls=%async_computation.2 | async-start | bytes 2097152 | tf_op jit(solution)/shard_map/all_to_all | solution.py:373
  114.3 12.3 %collective-permute-start.8 = (f32[128,4096]{1,0:T(8,128)}, f32[128,4096]{1,0:T(8,128)}, u32[]{:S(2)}, u32[]{:S(2)}) collective-permute-start(f32[128,4096]{1,0:T(8,128)} %get-tuple-element.49), channel_id=1, source_target_pairs={{0,1},{1,0},{2,3},{3,2},{4,5},{5,4},{6,7},{7,6},{8,9},{9,8},{10,11... | collective-permute-start | bytes 6291464 | tf_op jit(solution)/shard_map/ppermute | solution.py:395
  116.5 14.3 %copy-start.1 = (f32[128,4096]{1,0:T(8,128)S(1)}, f32[128,4096]{1,0:T(8,128)}, u32[]{:S(2)}) copy-start(f32[128,4096]{1,0:T(8,128)} %get-tuple-element.48.refs_0_) | copy-start | bytes 6291460
  126.6 4.2 %collective-permute-start.10 = (f32[128,4096]{1,0:T(8,128)S(1)}, f32[128,4096]{1,0:T(8,128)S(1)}, u32[]{:S(2)}, u32[]{:S(2)}) collective-permute-start(f32[128,4096]{1,0:T(8,128)S(1)} %get-tuple-element.56), channel_id=1, source_target_pairs={{0,1},{1,0},{2,3},{3,2},{4,5},{5,4},{6,7},{7,6},{8,9},{9,8},{10,11... | collective-permute-start | bytes 6291464 | tf_op jit(solution)/shard_map/ppermute | solution.py:395
